TPU v7x, 32 devices: a whole 2x2x4 slice. The times are simulated.
32 devices in a mesh: section: 2 (over x), expert: 4 (over y, core), dp: 4 (over z).
Axes of the slice: x: 2, y: 2, z: 4, core: 2. Of those that a mesh axis runs over, the one named last changes fastest.
Arguments:
- inputs: bfloat16 [4, 512, 3072], P(None, ('expert', 'dp')), may hold values from -6 to 6
- upstream: bfloat16 [4, 512, 3072], P(None, ('expert', 'dp')), may hold values from -1.5 to 1.5
- route_mask: int32 [2, 4, 512], P('section', None, ('expert', 'dp')), may hold values from 0 to 1, as said below
- route_weights: float32 [2, 4, 512], P('section', None, ('expert', 'dp')), may hold values from 0.2 to 1
- gate_weight: bfloat16 [2, 3072, 8192], P('section', None, ('expert', 'dp')), may hold values from -0.109375 to 0.109375
- up_weight: bfloat16 [2, 3072, 8192], P('section', None, ('expert', 'dp')), may hold values from -0.109375 to 0.109375
- down_weight: bfloat16 [2, 8192, 3072], P('section', ('expert', 'dp')), may hold values from -0.0625 to 0.0625
Outputs:
- gate_grad: bfloat16 [2, 3072, 8192], P('section', None, ('expert', 'dp'))
- up_grad: bfloat16 [2, 3072, 8192], P('section', None, ('expert', 'dp'))
- down_grad: bfloat16 [2, 8192, 3072], P('section', ('expert', 'dp'))
Inputs may be any that keep to these rules, and one draw needn't show every extreme that they name: `route_mask`: in each layer and micro-batch, each aligned block of 32 tokens (the tokens of one device) has at most 8 ones, and some block exactly 8.
All inputs are finite; a program needn't handle non-finite values.
Results may differ from a plain program's by a relative error of at most 0.0095.
Values may be sent and summed in bfloat16 or wider, within the bound.
A program may use at most 128 MiB of HBM per device.

v0:
```python
import jax
import jax.numpy as jnp
from jax import lax
from jax.sharding import PartitionSpec as P

CAP = 8


EPSILON = 1e-05


def shifted(block, axis, distance):
    devices = range(lax.axis_size(axis))
    route = [(i - distance, i) for i in devices if i - distance in devices]
    return lax.ppermute(block, axis, route)


def normalize(layer_input):
    input_f = layer_input.astype(jnp.float32)
    scale = lax.rsqrt(jnp.mean(input_f * input_f, axis=-1, keepdims=True) + EPSILON)
    return (input_f, scale, (input_f * scale).astype(jnp.bfloat16))


def slot_table(mask_row):
    position = jnp.cumsum(mask_row) - 1
    chosen = (mask_row[:, None] == 1) & (
        position[:, None] == jnp.arange(CAP, dtype=jnp.int32)[None, :]
    )
    return chosen.astype(jnp.bfloat16)


def pick_rows(table, values):
    return lax.dot_general(
        table, values, (((0,), (0,)), ((), ())), preferred_element_type=jnp.float32
    ).astype(jnp.bfloat16)


def layer_forward(layer_input, mask_row, weight_row, gate_w, up_w, down_w):
    input_f, scale, normed = normalize(layer_input)
    table = slot_table(mask_row)
    send_rows = pick_rows(table, normed)
    rows = lax.all_gather(send_rows, ("expert", "dp"), axis=0, tiled=True)
    gate_pre = jnp.dot(rows, gate_w, preferred_element_type=jnp.float32)
    up_pre = jnp.dot(rows, up_w, preferred_element_type=jnp.float32)
    hidden = (jax.nn.silu(gate_pre) * up_pre).astype(jnp.bfloat16)
    summed = lax.psum_scatter(
        jnp.dot(hidden, down_w, preferred_element_type=jnp.float32).astype(jnp.bfloat16),
        ("expert", "dp"),
        scatter_dimension=0,
        tiled=True,
    )
    back = jnp.dot(table, summed, preferred_element_type=jnp.float32)
    output = (input_f + weight_row[:, None] * back).astype(jnp.bfloat16)
    return (output, rows)


def layer_backward(layer_input, mask_row, weight_row, gate_w, up_w, down_w, flowing):
    contract_rows = (((1,), (1,)), ((), ()))
    input_f, scale, normed = normalize(layer_input)
    table = slot_table(mask_row)
    flowing_f = flowing.astype(jnp.float32)
    out_grad = (weight_row[:, None] * flowing_f).astype(jnp.bfloat16)
    send_grad = pick_rows(table, out_grad)
    send_rows = pick_rows(table, normed)
    rows, grad_rows = (
        lax.all_gather(send_rows, ("expert", "dp"), axis=0, tiled=True),
        lax.all_gather(send_grad, ("expert", "dp"), axis=0, tiled=True),
    )
    gate_pre = jnp.dot(rows, gate_w, preferred_element_type=jnp.float32)
    up_pre = jnp.dot(rows, up_w, preferred_element_type=jnp.float32)
    sigma = jax.nn.sigmoid(gate_pre)
    silu_val = jax.nn.silu(gate_pre)
    hidden = (silu_val * up_pre).astype(jnp.bfloat16)
    hidden_grad = lax.dot_general(
        grad_rows, down_w, contract_rows, preferred_element_type=jnp.float32
    )
    gate_pre_grad = (hidden_grad * up_pre * sigma * (1.0 + gate_pre * (1.0 - sigma))).astype(
        jnp.bfloat16
    )
    up_pre_grad = (hidden_grad * silu_val).astype(jnp.bfloat16)
    summed = lax.psum_scatter(
        (
            lax.dot_general(
                gate_pre_grad, gate_w, contract_rows, preferred_element_type=jnp.float32
            )
            + lax.dot_general(up_pre_grad, up_w, contract_rows, preferred_element_type=jnp.float32)
        ).astype(jnp.bfloat16),
        ("expert", "dp"),
        scatter_dimension=0,
        tiled=True,
    )
    total = jnp.dot(table, summed, preferred_element_type=jnp.float32)
    inner = jnp.mean(input_f * total, axis=-1, keepdims=True)
    input_grad = (flowing_f + scale * total - input_f * (scale * scale * scale) * inner).astype(
        jnp.bfloat16
    )
    units = jnp.stack([hidden, gate_pre_grad, up_pre_grad])
    return (input_grad, rows, grad_rows, units)


def store_if(store, index, value, valid):
    older = lax.dynamic_index_in_dim(store, index, 0, keepdims=False)
    return store.at[index].set(jnp.where(valid, value, older))


def shards(inputs, upstream, route_mask, route_weights, gate_weight, up_weight, down_weight):
    sections = lax.axis_size("section")
    section = lax.axis_index("section")
    micro_count = inputs.shape[0]
    token_count = inputs.shape[1]
    model_width = inputs.shape[2]
    hidden_width = gate_weight.shape[2]
    group_rows = lax.axis_size(("expert", "dp")) * CAP
    ticks = micro_count + sections - 1
    gate_w = gate_weight[0]
    up_w = up_weight[0]
    down_w = down_weight[0]
    masks = route_mask[0]
    weights = route_weights[0]
    stash_inputs = jnp.zeros((micro_count, token_count, model_width), jnp.bfloat16)
    stash_rows = jnp.zeros((1,), jnp.bfloat16)

    def forward_tick(tick, carry):
        incoming, stash_inputs, stash_rows = carry
        micro_index = tick - section
        valid = (micro_index >= 0) & (micro_index < micro_count)
        clipped = jnp.clip(micro_index, 0, micro_count - 1)
        first_input = lax.dynamic_index_in_dim(inputs, clipped, 0, keepdims=False)
        current = jnp.where(section == 0, first_input, incoming)
        mask_row = lax.dynamic_index_in_dim(masks, clipped, 0, keepdims=False)
        weight_row = lax.dynamic_index_in_dim(weights, clipped, 0, keepdims=False)
        stash_inputs = store_if(stash_inputs, clipped, current, valid)
        output, rows = layer_forward(current, mask_row, weight_row, gate_w, up_w, down_w)
        finished = jnp.where(valid, output, jnp.zeros_like(output))
        incoming = shifted(finished, "section", 1)
        return (incoming, stash_inputs, stash_rows)

    start = jnp.zeros((token_count, model_width), jnp.bfloat16)
    unused, stash_inputs, stash_rows = lax.fori_loop(
        0, ticks, forward_tick, (start, stash_inputs, stash_rows)
    )
    rows_store = jnp.zeros((micro_count, group_rows, model_width), jnp.bfloat16)
    grads_store = jnp.zeros((micro_count, group_rows, model_width), jnp.bfloat16)
    units_store = jnp.zeros((micro_count, 3, group_rows, hidden_width), jnp.bfloat16)

    def backward_tick(tick, carry):
        incoming, rows_store, grads_store, units_store = carry
        micro_index = tick - (sections - 1 - section)
        valid = (micro_index >= 0) & (micro_index < micro_count)
        clipped = jnp.clip(micro_index, 0, micro_count - 1)
        last_grad = lax.dynamic_index_in_dim(upstream, clipped, 0, keepdims=False)
        current = jnp.where(section == sections - 1, last_grad, incoming)
        mask_row = lax.dynamic_index_in_dim(masks, clipped, 0, keepdims=False)
        weight_row = lax.dynamic_index_in_dim(weights, clipped, 0, keepdims=False)
        layer_input = lax.dynamic_index_in_dim(stash_inputs, clipped, 0, keepdims=False)
        input_grad, rows, grad_rows, units = layer_backward(
            layer_input, mask_row, weight_row, gate_w, up_w, down_w, current
        )
        rows_store = store_if(rows_store, clipped, rows, valid)
        grads_store = store_if(grads_store, clipped, grad_rows, valid)
        units_store = store_if(units_store, clipped, units, valid)
        finished = jnp.where(valid, input_grad, jnp.zeros_like(input_grad))
        incoming = shifted(finished, "section", -1)
        return (incoming, rows_store, grads_store, units_store)

    unused, rows_store, grads_store, units_store = lax.fori_loop(
        0, ticks, backward_tick, (start, rows_store, grads_store, units_store)
    )
    all_rows = rows_store.reshape(-1, model_width)
    all_grads = grads_store.reshape(-1, model_width)
    hidden_all = units_store[:, 0].reshape(-1, hidden_width)
    gate_all = units_store[:, 1].reshape(-1, hidden_width)
    up_all = units_store[:, 2].reshape(-1, hidden_width)
    contract_first = (((0,), (0,)), ((), ()))
    gate_grad = lax.dot_general(
        all_rows, gate_all, contract_first, preferred_element_type=jnp.float32
    )
    up_grad = lax.dot_general(all_rows, up_all, contract_first, preferred_element_type=jnp.float32)
    down_grad = lax.dot_general(
        hidden_all, all_grads, contract_first, preferred_element_type=jnp.float32
    )
    return (
        gate_grad.astype(jnp.bfloat16)[None],
        up_grad.astype(jnp.bfloat16)[None],
        down_grad.astype(jnp.bfloat16)[None],
    )


def solution(mesh):
    return jax.shard_map(
        shards,
        mesh=mesh,
        in_specs=(
            P(None, ("expert", "dp"), None),
            P(None, ("expert", "dp"), None),
            P("section", None, ("expert", "dp")),
            P("section", None, ("expert", "dp")),
            P("section", None, ("expert", "dp")),
            P("section", None, ("expert", "dp")),
            P("section", ("expert", "dp"), None),
        ),
        out_specs=(
            P("section", None, ("expert", "dp")),
            P("section", None, ("expert", "dp")),
            P("section", ("expert", "dp"), None),
        ),
        check_vma=False,
    )
```

profile of v0, /device:TPU:0, one launch (start us, length us, event | category | flops | bytes accessed | tf_op | source)
XLA Modules:
  0.0 1395.9 jit_solution(2319598621400494459)
XLA Ops:
  8.2 588.0 %while.42 = (s32[]{:T(128)}, bf16[32,3072]{1,0:T(8,128)(2,1)S(1)}, bf16[4,32,3072]{2,1,0:T(8,128)(2,1)}, s32[]{:T(128)}, pred[]{:T(512)}, /*index=5*/bf16[4,32,3...) while((s32[]{:T(128)}, bf16[32,3072]{1,0:T(8,128)(2,1)S(1)}, ...), condition=%wide.region_5.6_spmd, body=%wide.region_0.5_spmd.sunk | while | flops 1213294720 | bytes 35229956 | solution.py:139
  15.2 41.6 %all_gather.33 = bf16[128,3072]{1,0:T(8,128)(2,1)S(1)} all-gather(bf16[8,3072]{1,0:T(8,128)(2,1)S(1)} %convolution_convert_fusion.11), channel_id=1, replica_groups=mesh['section'=2,'expert'=4,'dp'=4] {'expert','dp'}, dimensions={0}, use_global_device_ids=true | all-gather | bytes 835584 | tf_op jit(solution)/shard_map/while/body/eval_jaxpr/all_gather | solution.py:42
  65.0 54.6 %reduce-scatter.3.cloned.1.call-done = bf16[8,3072]{1,0:T(8,128)(2,1)} async-done(((bf16[128,3072]{1,0:T(8,128)(2,1)}), bf16[8,3072]{1,0:T(8,128)(2,1)}) %reduce-scatter.3.cloned.1.call-update) | async-done | bytes 49168 | tf_op jit(solution)/shard_map/while/body/eval_jaxpr/reduce_scatter | solution.py:46
  134.4 39.9 %all_gather.33 = bf16[128,3072]{1,0:T(8,128)(2,1)S(1)} all-gather(bf16[8,3072]{1,0:T(8,128)(2,1)S(1)} %convolution_convert_fusion.11), channel_id=1, replica_groups=mesh['section'=2,'expert'=4,'dp'=4] {'expert','dp'}, dimensions={0}, use_global_device_ids=true | all-gather | bytes 835584 | tf_op jit(solution)/shard_map/while/body/eval_jaxpr/all_gather | solution.py:42
  182.6 54.2 %reduce-scatter.3.cloned.1.call-done = bf16[8,3072]{1,0:T(8,128)(2,1)} async-done(((bf16[128,3072]{1,0:T(8,128)(2,1)}), bf16[8,3072]{1,0:T(8,128)(2,1)}) %reduce-scatter.3.cloned.1.call-update) | async-done | bytes 49168 | tf_op jit(solution)/shard_map/while/body/eval_jaxpr/reduce_scatter | solution.py:46
  251.6 39.8 %all_gather.33 = bf16[128,3072]{1,0:T(8,128)(2,1)S(1)} all-gather(bf16[8,3072]{1,0:T(8,128)(2,1)S(1)} %convolution_convert_fusion.11), channel_id=1, replica_groups=mesh['section'=2,'expert'=4,'dp'=4] {'expert','dp'}, dimensions={0}, use_global_device_ids=true | all-gather | bytes 835584 | tf_op jit(solution)/shard_map/while/body/eval_jaxpr/all_gather | solution.py:42
  299.6 54.2 %reduce-scatter.3.cloned.1.call-done = bf16[8,3072]{1,0:T(8,128)(2,1)} async-done(((bf16[128,3072]{1,0:T(8,128)(2,1)}), bf16[8,3072]{1,0:T(8,128)(2,1)}) %reduce-scatter.3.cloned.1.call-update) | async-done | bytes 49168 | tf_op jit(solution)/shard_map/while/body/eval_jaxpr/reduce_scatter | solution.py:46
  368.7 40.0 %all_gather.33 = bf16[128,3072]{1,0:T(8,128)(2,1)S(1)} all-gather(bf16[8,3072]{1,0:T(8,128)(2,1)S(1)} %convolution_convert_fusion.11), channel_id=1, replica_groups=mesh['section'=2,'expert'=4,'dp'=4] {'expert','dp'}, dimensions={0}, use_global_device_ids=true | all-gather | bytes 835584 | tf_op jit(solution)/shard_map/while/body/eval_jaxpr/all_gather | solution.py:42
  416.9 54.2 %reduce-scatter.3.cloned.1.call-done = bf16[8,3072]{1,0:T(8,128)(2,1)} async-done(((bf16[128,3072]{1,0:T(8,128)(2,1)}), bf16[8,3072]{1,0:T(8,128)(2,1)}) %reduce-scatter.3.cloned.1.call-update) | async-done | bytes 49168 | tf_op jit(solution)/shard_map/while/body/eval_jaxpr/reduce_scatter | solution.py:46
  486.0 40.0 %all_gather.33 = bf16[128,3072]{1,0:T(8,128)(2,1)S(1)} all-gather(bf16[8,3072]{1,0:T(8,128)(2,1)S(1)} %convolution_convert_fusion.11), channel_id=1, replica_groups=mesh['section'=2,'expert'=4,'dp'=4] {'expert','dp'}, dimensions={0}, use_global_device_ids=true | all-gather | bytes 835584 | tf_op jit(solution)/shard_map/while/body/eval_jaxpr/all_gather | solution.py:42
  534.2 54.2 %reduce-scatter.3.cloned.1.call-done = bf16[8,3072]{1,0:T(8,128)(2,1)} async-done(((bf16[128,3072]{1,0:T(8,128)(2,1)}), bf16[8,3072]{1,0:T(8,128)(2,1)}) %reduce-scatter.3.cloned.1.call-update) | async-done | bytes 49168 | tf_op jit(solution)/shard_map/while/body/eval_jaxpr/reduce_scatter | solution.py:46
  602.2 772.7 %while.43 = (s32[]{:T(128)}, bf16[32,3072]{1,0:T(8,128)(2,1)}, bf16[4,128,3072]{2,1,0:T(8,128)(2,1)}, bf16[4,128,3072]{2,1,0:T(8,128)(2,1)}, bf16[4,3,128,512]{3...) while((s32[]{:T(128)}, bf16[32,3072]{1,0:T(8,128)(2,1)}, ...), condition=%wide.region_13.14_spmd, body=%wide.region_6.13_spmd.sunk | while | flops 2025212544 | bytes 78193088 | solution.py:166
  607.5 40.1 %all_gather.34 = bf16[128,3072]{1,0:T(8,128)(2,1)S(1)} all-gather(bf16[8,3072]{1,0:T(8,128)(2,1)S(1)} %convolution_convert_fusion.13), channel_id=1, replica_groups=mesh['section'=2,'expert'=4,'dp'=4] {'expert','dp'}, dimensions={0}, use_global_device_ids=true | all-gather | bytes 835584 | tf_op jit(solution)/shard_map/while/body/eval_jaxpr/all_gather | solution.py:66
  696.4 51.1 %reduce-scatter.5.cloned.1.call-done = bf16[8,3072]{1,0:T(8,128)(2,1)} async-done(((bf16[128,3072]{1,0:T(8,128)(2,1)}), bf16[8,3072]{1,0:T(8,128)(2,1)}) %reduce-scatter.5.cloned.1.call-update) | async-done | bytes 49168 | tf_op jit(solution)/shard_map/while/body/eval_jaxpr/reduce_scatter | solution.py:81
  763.0 40.2 %all_gather.34 = bf16[128,3072]{1,0:T(8,128)(2,1)S(1)} all-gather(bf16[8,3072]{1,0:T(8,128)(2,1)S(1)} %convolution_convert_fusion.13), channel_id=1, replica_groups=mesh['section'=2,'expert'=4,'dp'=4] {'expert','dp'}, dimensions={0}, use_global_device_ids=true | all-gather | bytes 835584 | tf_op jit(solution)/shard_map/while/body/eval_jaxpr/all_gather | solution.py:66
  852.1 49.7 %reduce-scatter.5.cloned.1.call-done = bf16[8,3072]{1,0:T(8,128)(2,1)} async-done(((bf16[128,3072]{1,0:T(8,128)(2,1)}), bf16[8,3072]{1,0:T(8,128)(2,1)}) %reduce-scatter.5.cloned.1.call-update) | async-done | bytes 49168 | tf_op jit(solution)/shard_map/while/body/eval_jaxpr/reduce_scatter | solution.py:81
  917.3 39.7 %all_gather.34 = bf16[128,3072]{1,0:T(8,128)(2,1)S(1)} all-gather(bf16[8,3072]{1,0:T(8,128)(2,1)S(1)} %convolution_convert_fusion.13), channel_id=1, replica_groups=mesh['section'=2,'expert'=4,'dp'=4] {'expert','dp'}, dimensions={0}, use_global_device_ids=true | all-gather | bytes 835584 | tf_op jit(solution)/shard_map/while/body/eval_jaxpr/all_gather | solution.py:66
  958.6 35.3 %all_gather.35 = bf16[128,3072]{1,0:T(8,128)(2,1)S(1)} all-gather(bf16[8,3072]{1,0:T(8,128)(2,1)S(1)} %convolution_convert_fusion.14), channel_id=1, replica_groups=mesh['section'=2,'expert'=4,'dp'=4] {'expert','dp'}, dimensions={0}, use_global_device_ids=true | all-gather | bytes 835584 | tf_op jit(solution)/shard_map/while/body/eval_jaxpr/all_gather | solution.py:67
  1006.0 49.7 %reduce-scatter.5.cloned.1.call-done = bf16[8,3072]{1,0:T(8,128)(2,1)} async-done(((bf16[128,3072]{1,0:T(8,128)(2,1)}), bf16[8,3072]{1,0:T(8,128)(2,1)}) %reduce-scatter.5.cloned.1.call-update) | async-done | bytes 49168 | tf_op jit(solution)/shard_map/while/body/eval_jaxpr/reduce_scatter | solution.py:81
  1071.2 40.1 %all_gather.34 = bf16[128,3072]{1,0:T(8,128)(2,1)S(1)} all-gather(bf16[8,3072]{1,0:T(8,128)(2,1)S(1)} %convolution_convert_fusion.13), channel_id=1, replica_groups=mesh['section'=2,'expert'=4,'dp'=4] {'expert','dp'}, dimensions={0}, use_global_device_ids=true | all-gather | bytes 835584 | tf_op jit(solution)/shard_map/while/body/eval_jaxpr/all_gather | solution.py:66
  1112.9 35.3 %all_gather.35 = bf16[128,3072]{1,0:T(8,128)(2,1)S(1)} all-gather(bf16[8,3072]{1,0:T(8,128)(2,1)S(1)} %convolution_convert_fusion.14), channel_id=1, replica_groups=mesh['section'=2,'expert'=4,'dp'=4] {'expert','dp'}, dimensions={0}, use_global_device_ids=true | all-gather | bytes 835584 | tf_op jit(solution)/shard_map/while/body/eval_jaxpr/all_gather | solution.py:67
  1160.3 49.8 %reduce-scatter.5.cloned.1.call-done = bf16[8,3072]{1,0:T(8,128)(2,1)} async-done(((bf16[128,3072]{1,0:T(8,128)(2,1)}), bf16[8,3072]{1,0:T(8,128)(2,1)}) %reduce-scatter.5.cloned.1.call-update) | async-done | bytes 49168 | tf_op jit(solution)/shard_map/while/body/eval_jaxpr/reduce_scatter | solution.py:81
  1225.7 40.2 %all_gather.34 = bf16[128,3072]{1,0:T(8,128)(2,1)S(1)} all-gather(bf16[8,3072]{1,0:T(8,128)(2,1)S(1)} %convolution_convert_fusion.13), channel_id=1, replica_groups=mesh['section'=2,'expert'=4,'dp'=4] {'expert','dp'}, dimensions={0}, use_global_device_ids=true | all-gather | bytes 835584 | tf_op jit(solution)/shard_map/while/body/eval_jaxpr/all_gather | solution.py:66
  1314.8 49.8 %reduce-scatter.5.cloned.1.call-done = bf16[8,3072]{1,0:T(8,128)(2,1)} async-done(((bf16[128,3072]{1,0:T(8,128)(2,1)}), bf16[8,3072]{1,0:T(8,128)(2,1)}) %reduce-scatter.5.cloned.1.call-update) | async-done | bytes 49168 | tf_op jit(solution)/shard_map/while/body/eval_jaxpr/reduce_scatter | solution.py:81
  (344 shorter events, 387.2 us)
Async XLA Ops:
  8.2 111.4 %reduce-scatter.3.cloned.1.call-start = ((), (), s32[]{:S(2)}) async-start(), calls=%async_computation.2 | async-start | bytes 835584 | tf_op jit(solution)/shard_map/while/body/eval_jaxpr/reduce_scatter | solution.py:46
  120.8 6.5 collective-permute-start
  127.4 109.4 %reduce-scatter.3.cloned.1.call-start = ((), (), s32[]{:S(2)}) async-start(), calls=%async_computation.2 | async-start | bytes 835584 | tf_op jit(solution)/shard_map/while/body/eval_jaxpr/reduce_scatter | solution.py:46
  238.0 6.6 collective-permute-start
  244.6 109.3 %reduce-scatter.3.cloned.1.call-start = ((), (), s32[]{:S(2)}) async-start(), calls=%async_computation.2 | async-start | bytes 835584 | tf_op jit(solution)/shard_map/while/body/eval_jaxpr/reduce_scatter | solution.py:46
  355.1 6.5 collective-permute-start
  361.6 109.5 %reduce-scatter.3.cloned.1.call-start = ((), (), s32[]{:S(2)}) async-start(), calls=%async_computation.2 | async-start | bytes 835584 | tf_op jit(solution)/shard_map/while/body/eval_jaxpr/reduce_scatter | solution.py:46
  472.3 6.6 collective-permute-start
  478.9 109.5 %reduce-scatter.3.cloned.1.call-start = ((), (), s32[]{:S(2)}) async-start(), calls=%async_computation.2 | async-start | bytes 835584 | tf_op jit(solution)/shard_map/while/body/eval_jaxpr/reduce_scatter | solution.py:46
  589.6 6.6 collective-permute-start
  602.2 145.3 %reduce-scatter.5.cloned.1.call-start = ((), (), s32[]{:S(2)}) async-start(), calls=%async_computation.3 | async-start | bytes 835584 | tf_op jit(solution)/shard_map/while/body/eval_jaxpr/reduce_scatter | solution.py:81
  607.4 77.5 %copy-start.3 = (bf16[512,3072]{1,0:T(8,128)(2,1)S(1)}, bf16[512,3072]{1,0:T(8,128)(2,1)}, u32[]{:S(2)}) copy-start(bf16[512,3072]{1,0:T(8,128)(2,1)} %get-tuple-element.1002) | copy-start | bytes 9437188 | tf_op jit(solution)/shard_map/while
  750.1 7.7 collective-permute-start.1
  757.8 144.0 %reduce-scatter.5.cloned.1.call-start = ((), (), s32[]{:S(2)}) async-start(), calls=%async_computation.3 | async-start | bytes 835584 | tf_op jit(solution)/shard_map/while/body/eval_jaxpr/reduce_scatter | solution.py:81
  763.0 77.6 %copy-start.3 = (bf16[512,3072]{1,0:T(8,128)(2,1)S(1)}, bf16[512,3072]{1,0:T(8,128)(2,1)}, u32[]{:S(2)}) copy-start(bf16[512,3072]{1,0:T(8,128)(2,1)} %get-tuple-element.1002) | copy-start | bytes 9437188 | tf_op jit(solution)/shard_map/while
  904.4 7.7 collective-permute-start.1
  912.1 143.6 %reduce-scatter.5.cloned.1.call-start = ((), (), s32[]{:S(2)}) async-start(), calls=%async_computation.3 | async-start | bytes 835584 | tf_op jit(solution)/shard_map/while/body/eval_jaxpr/reduce_scatter | solution.py:81
  1058.4 7.7 collective-permute-start.1
  1066.0 144.1 %reduce-scatter.5.cloned.1.call-start = ((), (), s32[]{:S(2)}) async-start(), calls=%async_computation.3 | async-start | bytes 835584 | tf_op jit(solution)/shard_map/while/body/eval_jaxpr/reduce_scatter | solution.py:81
  1071.2 77.6 %copy-start.3 = (bf16[512,3072]{1,0:T(8,128)(2,1)S(1)}, bf16[512,3072]{1,0:T(8,128)(2,1)}, u32[]{:S(2)}) copy-start(bf16[512,3072]{1,0:T(8,128)(2,1)} %get-tuple-element.1002) | copy-start | bytes 9437188 | tf_op jit(solution)/shard_map/while
  1212.8 7.7 collective-permute-start.1
  1220.5 144.2 %reduce-scatter.5.cloned.1.call-start = ((), (), s32[]{:S(2)}) async-start(), calls=%async_computation.3 | async-start | bytes 835584 | tf_op jit(solution)/shard_map/while/body/eval_jaxpr/reduce_scatter | solution.py:81
  1225.7 77.7 %copy-start.3 = (bf16[512,3072]{1,0:T(8,128)(2,1)S(1)}, bf16[512,3072]{1,0:T(8,128)(2,1)}, u32[]{:S(2)}) copy-start(bf16[512,3072]{1,0:T(8,128)(2,1)} %get-tuple-element.1002) | copy-start | bytes 9437188 | tf_op jit(solution)/shard_map/while
  1367.3 7.7 collective-permute-start.1
  (44 other events, 775.8 us)
Sparse Core Ops, SparseCore 0:
  64.5 55.1 reduce-scatter.2
  182.0 54.7 reduce-scatter.2
  299.1 54.7 reduce-scatter.2
  416.4 54.7 reduce-scatter.2
  533.6 54.7 reduce-scatter.2
  690.9 56.5 reduce-scatter.4
  846.5 55.2 reduce-scatter.4
  1000.4 55.2 reduce-scatter.4
  1154.8 55.3 reduce-scatter.4
  1309.3 55.3 reduce-scatter.4
where the time goes:
time: 1400 us
  blocking collectives  578 us (41%)
  waiting for transfers between devices  550 us (39%)
  matrix products  102 us (7%)
  other arithmetic  84.4 us (6%)
  local copies, waits for them, and re-layouts  43.7 us (3%)
  starting transfers between devices  23.4 us (2%)
  between operations  14 us (1%)
    reduce_scatter x5, waiting for transfers between devices, layer_forward(): lax.psum_scatter(jnp.dot(hidden, down_w, preferred_element_type=jnp.float...  271 us
    reduce_scatter x5, waiting for transfers between devices, layer_backward(): lax.psum_scatter((lax.dot_general(gate_pre_grad, gate_w, contract_rows, p...  250 us
    all_gather x5, blocking collectives, layer_forward(): rows = lax.all_gather(send_rows, ('expert', 'dp'), axis=0, tiled=True)  201 us
    all_gather x5, blocking collectives, layer_backward(): lax.all_gather(send_rows, ('expert', 'dp'), axis=0, tiled=True)  200 us
    all_gather x5, blocking collectives, layer_backward(): lax.all_gather(send_grad, ('expert', 'dp'), axis=0, tiled=True)  176 us
    scatter x20, other arithmetic, store_if(): return store.at[index].set(jnp.where(valid, value, older))  42.4 us
  transfers between devices with their start and end apart: 20, of which 20 were waited for; matrix products, arithmetic and copies ran while one was open for 4% of the time, Pallas kernels for 0%

commit v1 on v0

v1 whole, which is shorter than its diff:
```python
import jax
import jax.numpy as jnp
from jax import lax
from jax.sharding import PartitionSpec as P

CAP = 8

EPSILON = 1e-05

GROUP = ("expert", "dp")


def slot_tables(mask):
    position = jnp.cumsum(mask, axis=1) - 1
    chosen = (mask[:, :, None] == 1) & (
        position[:, :, None] == jnp.arange(CAP, dtype=jnp.int32)[None, None, :]
    )
    return chosen.astype(jnp.bfloat16)


def pick(table, values):
    return lax.dot_general(
        table, values, (((1,), (1,)), ((0,), (0,))), preferred_element_type=jnp.float32
    ).astype(values.dtype)


def place(table, mask, rows, values):
    spread = lax.dot_general(
        table, rows, (((2,), (1,)), ((0,), (0,))), preferred_element_type=jnp.float32
    ).astype(values.dtype)
    return jnp.where(mask[:, :, None] == 1, spread, values)


def row_scale(rows_f):
    return lax.rsqrt(jnp.mean(rows_f * rows_f, axis=-1, keepdims=True) + EPSILON)


def gather(block):
    flat = block.reshape(-1, block.shape[-1])
    return lax.all_gather(flat, GROUP, axis=0, tiled=True)


def scatter_sum(partial, like):
    summed = lax.psum_scatter(partial, GROUP, scatter_dimension=0, tiled=True)
    return summed.reshape(like.shape)


def mm(a, b, dims=((1,), (0,))):
    return lax.dot_general(a, b, (dims, ((), ())), preferred_element_type=jnp.float32)


def shards(inputs, upstream, route_mask, route_weights, gate_weight, up_weight, down_weight):
    sections = lax.axis_size("section")
    section = lax.axis_index("section")
    gate_w, up_w, down_w = gate_weight[0], up_weight[0], down_weight[0]
    mask = route_mask[0]
    table = slot_tables(mask)
    weights = jnp.sum(table.astype(jnp.float32) * route_weights[0][:, :, None], axis=1)[:, :, None]
    up_route = [(i, i + 1) for i in range(sections - 1)]
    down_route = [(i + 1, i) for i in range(sections - 1)]
    next_table = lax.ppermute(table, "section", down_route)
    previous_table = lax.ppermute(table, "section", up_route)

    def activations(gate_pre, up_pre):
        return (jax.nn.silu(gate_pre) * up_pre).astype(jnp.bfloat16)

    def out_grad(g_rows):
        return (weights * g_rows.astype(jnp.float32)).astype(jnp.bfloat16)

    stream = inputs
    current = pick(table, inputs)
    last_rows = pick(table, upstream)
    grads_in = last_rows
    first_grad = out_grad(last_rows)
    is_last = section == sections - 1
    own = current
    all_rows = gate_pre = up_pre = all_grads = hidden_grad = None
    for t in range(sections):
        active = section == t
        own = jnp.where(active, current, own)
        own_f = current.astype(jnp.float32)
        normed = (own_f * row_scale(own_f)).astype(jnp.bfloat16)
        send = jnp.where(is_last, first_grad, normed) if t == 0 and sections > 1 else normed
        got = gather(send)
        if t == 0:
            all_grads = got if sections > 1 else gather(first_grad)
            hidden_grad = mm(all_grads, down_w, ((1,), (1,)))
            all_rows = got
            gate_pre = mm(got, gate_w)
            up_pre = mm(got, up_w)
            new_gate, new_up = gate_pre, up_pre
        else:
            new_gate, new_up = mm(got, gate_w), mm(got, up_w)
            all_rows = jnp.where(active, got, all_rows)
            gate_pre = jnp.where(active, new_gate, gate_pre)
            up_pre = jnp.where(active, new_up, up_pre)
        if t < sections - 1:
            partial = mm(activations(new_gate, new_up), down_w).astype(jnp.bfloat16)
            back = scatter_sum(partial, current).astype(jnp.float32)
            output_rows = (own_f + weights * back).astype(jnp.bfloat16)
            output = place(table, mask, output_rows, stream)
            if t == sections - 2:
                current = lax.ppermute(pick(next_table, output), "section", up_route)
            else:
                stream = lax.ppermute(output, "section", up_route)
                current = pick(table, stream)

    sigma = jax.nn.sigmoid(gate_pre)
    silu_val = jax.nn.silu(gate_pre)
    hidden = activations(gate_pre, up_pre)
    slope = up_pre * sigma * (1.0 + gate_pre * (1.0 - sigma))
    own_f = own.astype(jnp.float32)
    scale = row_scale(own_f)

    flow = upstream
    for t in reversed(range(sections)):
        active = section == t
        if t < sections - 1:
            got = gather(out_grad(grads_in))
            all_grads = jnp.where(active, got, all_grads)
            hidden_grad = mm(all_grads, down_w, ((1,), (1,)))
        gate_units = (hidden_grad * slope).astype(jnp.bfloat16)
        up_units = (hidden_grad * silu_val).astype(jnp.bfloat16)
        if t > 0:
            partial = mm(gate_units, gate_w, ((1,), (1,))) + mm(up_units, up_w, ((1,), (1,)))
            total = scatter_sum(partial.astype(jnp.bfloat16), own).astype(jnp.float32)
            inner = jnp.mean(own_f * total, axis=-1, keepdims=True)
            grad_rows = (
                grads_in.astype(jnp.float32)
                + scale * total
                - own_f * (scale * scale * scale) * inner
            ).astype(jnp.bfloat16)
            result = place(table, mask, grad_rows, flow)
            if t == 1:
                grads_in = lax.ppermute(pick(previous_table, result), "section", down_route)
            else:
                flow = lax.ppermute(result, "section", down_route)
                grads_in = pick(table, flow)

    gate_grad = mm(all_rows, gate_units, ((0,), (0,)))
    up_grad = mm(all_rows, up_units, ((0,), (0,)))
    down_grad = mm(hidden, all_grads, ((0,), (0,)))
    return (
        gate_grad.astype(jnp.bfloat16)[None],
        up_grad.astype(jnp.bfloat16)[None],
        down_grad.astype(jnp.bfloat16)[None],
    )


def solution(mesh):
    return jax.shard_map(
        shards,
        mesh=mesh,
        in_specs=(
            P(None, ("expert", "dp"), None),
            P(None, ("expert", "dp"), None),
            P("section", None, ("expert", "dp")),
            P("section", None, ("expert", "dp")),
            P("section", None, ("expert", "dp")),
            P("section", None, ("expert", "dp")),
            P("section", ("expert", "dp"), None),
        ),
        out_specs=(
            P("section", None, ("expert", "dp")),
            P("section", None, ("expert", "dp")),
            P("section", ("expert", "dp"), None),
        ),
        check_vma=False,
    )
```

time: 1400 us -> 354 us (0.25)
  blocking collectives: 578 us -> 0 us
  waiting for transfers between devices: 550 us -> 265 us
  other arithmetic: 84.4 us -> 8.43 us
  matrix products: 102 us -> 52 us
  local copies, waits for them, and re-layouts: 43.7 us -> 3.77 us
    all_gather x15 -> x0, blocking collectives: 578 us -> none  [the longest x5 201 us: layer_forward(): rows = lax.all_gather(send_rows, ('expert', 'dp'), axis=0, tiled=True)]
    reduce_scatter x10 -> x2, waiting for transfers between devices: 522 us -> 120 us  [scatter_sum(): summed = lax.psum_scatter(partial, GROUP, scatter_dimension=0, tiled=True)]
    all_gather x0 -> x3, waiting for transfers between devices: none -> 131 us  [gather(): return lax.all_gather(flat, GROUP, axis=0, tiled=True)]
    dot_general x63 -> x16, matrix products: 102 us -> 52 us  [the longest x12 43.4 us: mm(): lax.dot_general(a, b, (dims, ((), ())), preferred_element_type=jnp.float32)]
    scatter x20 -> x0, other arithmetic: 42.4 us -> none  [store_if(): return store.at[index].set(jnp.where(valid, value, older))]
    another operation x25 -> x1, other arithmetic: 18.2 us -> 0.94 us  [slot_tables(): position = jnp.cumsum(mask, axis=1) - 1]
  transfers between devices with their start and end apart: 20 -> 9, of which waited for: 20 -> 8; matrix products, arithmetic and copies ran while one was open for 4% -> 2% of each run, Pallas kernels for 0% -> 0%
where the time goes in v1:
time: 354 us; the launch traced here: 353 us
  waiting for transfers between devices  265 us (75%)
  matrix products  52 us (15%)
  between operations  14 us (4%)
  starting transfers between devices  9.78 us (3%)
  other arithmetic  8.43 us (2%)
  local copies, waits for them, and re-layouts  3.77 us (1%)
    all_gather x3, waiting for transfers between devices, gather(): return lax.all_gather(flat, GROUP, axis=0, tiled=True)  131 us
    reduce_scatter x2, waiting for transfers between devices, scatter_sum(): summed = lax.psum_scatter(partial, GROUP, scatter_dimension=0, tiled=True)  120 us
    dot_general x12, matrix products, mm(): lax.dot_general(a, b, (dims, ((), ())), preferred_element_type=jnp.float32)  43.4 us
    dot_general x4, matrix products, pick(): lax.dot_general(table, values, (((1,), (1,)), ((0,), (0,))), preferred_el...  8.57 us
  transfers between devices with their start and end apart: 9, of which 8 were waited for; matrix products, arithmetic and copies ran while one was open for 2% of the time, Pallas kernels for 0%

profile of v1, /device:TPU:0, one launch (start us, length us, event | category | flops | bytes accessed | tf_op | source)
XLA Modules:
  0.0 353.2 jit_solution(14080238198581466288)
XLA Ops:
  9.8 2.0 fusion.37
  15.0 48.0 %all-gather.4.cloned.1.call-done = bf16[512,3072]{1,0:T(8,128)(2,1)} async-done(((bf16[32,3072]{1,0:T(8,128)(2,1)}), bf16[512,3072]{1,0:T(8,128)(2,1)}) %all-gather.4.cloned.1.call-update) | async-done | bytes 3145744 | tf_op jit(solution)/shard_map/all_gather | solution.py:40
  63.0 4.8 %fusion.14 = f32[512,512]{1,0:T(8,128)S(1)} fusion(bf16[512,3072]{1,0:T(8,128)(2,1)} %all-gather.4.cloned.1.call-done, bf16[1,3072,512]{2,1,0:T(8,128)(2,1)} %param.12), kind=kOutput, calls=%fused_computation.25 | convolution fusion | flops 1610612736 | bytes 7340032 | tf_op jit(solution)/shard_map/dot_general | solution.py:49
  70.6 3.5 convolution_convert_fusion.3
  76.1 4.4 %collective-permute-done = bf16[4,32,8]{1,2,0:T(8,128)(2,1)} collective-permute-done((bf16[4,32,8]{1,2,0:T(8,128)(2,1)S(1)}, bf16[4,32,8]{1,2,0:T(8,128)(2,1)}, u32[]{:S(2)}, u32[]{:S(2)}) %collective-permute-start) | collective-permute-done | bytes 2080 | tf_op jit(solution)/shard_map/ppermute | solution.py:61
  80.4 58.9 %reduce-scatter.3.cloned.1.call-done = bf16[32,3072]{1,0:T(8,128)(2,1)} async-done(((bf16[512,3072]{1,0:T(8,128)(2,1)}), bf16[32,3072]{1,0:T(8,128)(2,1)}) %reduce-scatter.3.cloned.1.call-update) | async-done | bytes 196624 | tf_op jit(solution)/shard_map/reduce_scatter | solution.py:44
  139.3 2.6 convolution_convert_fusion.9
  141.9 3.4 collective-permute-start.1
  145.3 3.5 collective-permute-done.1
  150.3 5.6 %fusion.8 = f32[512,512]{1,0:T(8,128)} fusion(bf16[512,3072]{1,0:T(8,128)(2,1)} %all-gather.4.cloned.1.call-done, bf16[1,512,3072]{2,1,0:T(8,128)(2,1)} %param.13), kind=kOutput, calls=%fused_computation.19 | convolution fusion | flops 1610612736 | bytes 7340032 | tf_op jit(solution)/shard_map/dot_general | solution.py:49
  155.9 39.5 %all-gather.6.cloned.1.call-done = bf16[512,3072]{1,0:T(8,128)(2,1)} async-done(((bf16[32,3072]{1,0:T(8,128)(2,1)}), bf16[512,3072]{1,0:T(8,128)(2,1)}) %all-gather.6.cloned.1.call-update) | async-done | bytes 3145744 | tf_op jit(solution)/shard_map/all_gather | solution.py:40
  195.4 4.1 %fusion.22 = f32[512,512]{1,0:T(8,128)S(1)} fusion(f32[512,512]{1,0:T(8,128)} %copy-done.17, bf16[512,3072]{1,0:T(8,128)(2,1)} %all-gather.6.cloned.1.call-done, bf16[1,3072,512]{2,1,0:T(8,128)(2,1)S(1)} %copy-done, pred[]{:T(512)S(6)} %eq.31), kind=kOutput, calls=%fused_computation.35 | convolution fusion | flops 1610874880 | bytes 8388609 | tf_op jit(solution)/shard_map/dot_general | solution.py:49
  202.5 2.1 fusion.16
  204.6 3.6 %add_convert_fusion = bf16[512,3072]{1,0:T(8,128)(2,1)} fusion(f32[512,3072]{1,0:T(8,128)S(1)} %fusion.16, bf16[1,3072,512]{2,1,0:T(8,128)(2,1)S(1)} %copy-done.4, f32[512,512]{1,0:T(8,128)S(1)} %copy-done.3, f32[512,512]{1,0:T(8,128)S(1)} %fusion.22), kind=kOutput, calls=%fused_computation | convolution fusion | flops 1615331328 | bytes 14680064 | tf_op jit(solution)/shard_map/dot_general | solution.py:49
  208.3 3.7 %collective-permute-start.2 = (bf16[4,32,8]{1,2,0:T(8,128)(2,1)}, bf16[4,32,8]{1,2,0:T(8,128)(2,1)}, u32[]{:S(2)}, u32[]{:S(2)}) collective-permute-start(bf16[4,32,8]{1,2,0:T(8,128)(2,1)} %copy-done.8), channel_id=1, source_target_pairs={{0,16},{1,17},{2,18},{3,19},{4,20},{5,21},{6,22},{7,23},{8,24},{9,... | collective-permute-start | bytes 6152 | tf_op jit(solution)/shard_map/ppermute | solution.py:62
  211.9 61.2 %reduce-scatter.5.cloned.1.call-done = bf16[32,3072]{1,0:T(8,128)(2,1)} async-done(((bf16[512,3072]{1,0:T(8,128)(2,1)}), bf16[32,3072]{1,0:T(8,128)(2,1)}) %reduce-scatter.5.cloned.1.call-update) | async-done | bytes 196624 | tf_op jit(solution)/shard_map/reduce_scatter | solution.py:44
  273.1 1.8 fusion.40
  275.5 2.6 convolution_convert_fusion.8
  279.4 6.5 %collective-permute-done.3 = bf16[4,8,3072]{2,1,0:T(8,128)(2,1)S(1)} collective-permute-done((bf16[4,8,3072]{2,1,0:T(8,128)(2,1)}, bf16[4,8,3072]{2,1,0:T(8,128)(2,1)S(1)}, u32[]{:S(2)}, u32[]{:S(2)}) %collective-permute-start.3) | collective-permute-done | bytes 196640 | tf_op jit(solution)/shard_map/ppermute | solution.py:135
  286.7 43.3 %all-gather.8.cloned.1.call-done = bf16[512,3072]{1,0:T(8,128)(2,1)} async-done(((bf16[32,3072]{1,0:T(8,128)(2,1)}), bf16[512,3072]{1,0:T(8,128)(2,1)}) %all-gather.8.cloned.1.call-update) | async-done | bytes 3145744 | tf_op jit(solution)/shard_map/all_gather | solution.py:40
  330.0 4.8 %fusion.6 = f32[512,512]{1,0:T(8,128)S(1)} fusion(bf16[1,512,3072]{2,1,0:T(8,128)(2,1)} %param.13, bf16[512,3072]{1,0:T(8,128)(2,1)} %all-gather.8.cloned.1.call-done, bf16[512,3072]{1,0:T(8,128)(2,1)} %all-gather.4.cloned.1.call-done, pred[]{:T(512)S(6)} %eq.36), kind=kOutput, calls=%fused_computation.17 | convolution fusion | flops 1612185600 | bytes 10485761 | tf_op jit(solution)/shard_map/dot_general | solution.py:49
  335.3 3.7 %fusion.2 = bf16[1,512,3072]{2,1,0:T(8,128)(2,1)} fusion(bf16[512,3072]{1,0:T(8,128)(2,1)S(1)} %copy-done.14, bf16[512,3072]{1,0:T(8,128)(2,1)S(1)} %copy-done.11, pred[]{:T(512)S(6)} %eq.36, f32[512,512]{1,0:T(8,128)S(1)} %copy-done.6, f32[512,512]{1,0:T(8,128)S(1)} %copy-done.2), kind=kOutput, calls=%fused_computation.7 | convolution fusion | flops 1615331328 | bytes 11534337 | tf_op jit(solution)/shard_map/dot_general | solution.py:49
  339.0 3.8 %fusion = bf16[1,3072,512]{2,1,0:T(8,128)(2,1)} fusion(bf16[512,3072]{1,0:T(8,128)(2,1)S(1)} %copy-done.13, bf16[512,3072]{1,0:T(8,128)(2,1)S(1)} %copy-done.11, pred[]{:T(512)S(6)} %eq.31, f32[512,512]{1,0:T(8,128)S(1)} %fusion.6, f32[512,512]{1,0:T(8,128)S(1)} %copy-done.2, f32[512,512]{1,0:T(8,128)S(1)} %copy-done.6), kind=kOutput, calls=%fused_computation.5 | convolution fusion | flops 1616379904 | bytes 12582913 | tf_op jit(solution)/shard_map/dot_general | solution.py:49
  342.8 3.8 %fusion.1 = bf16[1,3072,512]{2,1,0:T(8,128)(2,1)} fusion(bf16[512,3072]{1,0:T(8,128)(2,1)S(1)} %copy-done.13, bf16[512,3072]{1,0:T(8,128)(2,1)S(1)} %copy-done.11, pred[]{:T(512)S(6)} %eq.31, f32[512,512]{1,0:T(8,128)S(1)} %fusion.6, f32[512,512]{1,0:T(8,128)S(1)} %copy-done.2), kind=kOutput, calls=%fused_computation.6 | convolution fusion | flops 1615331328 | bytes 11534337 | tf_op jit(solution)/shard_map/dot_general | solution.py:49
  (64 shorter events, 18.2 us)
Async XLA Ops:
  7.2 60.6 %copy-start = (bf16[1,3072,512]{2,1,0:T(8,128)(2,1)S(1)}, bf16[1,3072,512]{2,1,0:T(8,128)(2,1)}, u32[]{:S(2)}) copy-start(bf16[1,3072,512]{2,1,0:T(8,128)(2,1)} %param.11) | copy-start | bytes 9437188
  7.2 55.8 %all-gather.4.cloned.1.call-start = ((), (), s32[]{:S(2)}) async-start(), calls=%async_computation.2 | async-start | bytes 3342336 | tf_op jit(solution)/shard_map/all_gather | solution.py:40
  15.0 124.4 %reduce-scatter.3.cloned.1.call-start = ((), (), s32[]{:S(2)}) async-start(), calls=%async_computation.3 | async-start | bytes 3342336 | tf_op jit(solution)/shard_map/reduce_scatter | solution.py:44
  63.0 4.8 %copy-start.10 = (bf16[512,3072]{1,0:T(8,128)(2,1)S(1)}, bf16[512,3072]{1,0:T(8,128)(2,1)}, u32[]{:S(2)}) copy-start(bf16[512,3072]{1,0:T(8,128)(2,1)} %all-gather.4.cloned.1.call-done) | copy-start | bytes 9437188
  67.8 1.8 copy-start.15
  67.8 2.8 copy-start.9
  69.6 1.0 copy-start.17
  74.1 121.2 %all-gather.6.cloned.1.call-start = ((), (), s32[]{:S(2)}) async-start(), calls=%async_computation.4 | async-start | bytes 3342336 | tf_op jit(solution)/shard_map/all_gather | solution.py:40
  74.8 5.6 %collective-permute-start = (bf16[4,32,8]{1,2,0:T(8,128)(2,1)S(1)}, bf16[4,32,8]{1,2,0:T(8,128)(2,1)}, u32[]{:S(2)}, u32[]{:S(2)}) collective-permute-start(bf16[4,32,8]{1,2,0:T(8,128)(2,1)S(1)} %fusion.70), channel_id=1, source_target_pairs={{16,0},{17,1},{18,2},{19,3},{20,4},{21,5},{22,6},{23,7},{24,8},{25... | collective-permute-start | bytes 6152 | tf_op jit(solution)/shard_map/ppermute | solution.py:61
  141.9 6.8 %collective-permute-start.1 = (bf16[4,8,3072]{2,1,0:T(8,128)(2,1)}, bf16[4,8,3072]{2,1,0:T(8,128)(2,1)S(1)}, u32[]{:S(2)}, u32[]{:S(2)}) collective-permute-start(bf16[4,8,3072]{2,1,0:T(8,128)(2,1)} %convolution_convert_fusion.9), channel_id=1, source_target_pairs={{0,16},{1,17},{2,18},{3,19},{4,20},{5,21},{6,22},{7,23},{8,24},{9,... | collective-permute-start | bytes 589832 | tf_op jit(solution)/shard_map/ppermute | solution.py:103
  150.2 122.9 %reduce-scatter.5.cloned.1.call-start = ((), (), s32[]{:S(2)}) async-start(), calls=%async_computation.5 | async-start | bytes 3342336 | tf_op jit(solution)/shard_map/reduce_scatter | solution.py:44
  195.4 4.1 %copy-start.4 = (bf16[1,3072,512]{2,1,0:T(8,128)(2,1)S(1)}, bf16[1,3072,512]{2,1,0:T(8,128)(2,1)}, u32[]{:S(2)}) copy-start(bf16[1,3072,512]{2,1,0:T(8,128)(2,1)} %param.12) | copy-start | bytes 9437188
  195.4 4.1 %copy-start.12 = (bf16[512,3072]{1,0:T(8,128)(2,1)S(1)}, bf16[512,3072]{1,0:T(8,128)(2,1)}, u32[]{:S(2)}) copy-start(bf16[512,3072]{1,0:T(8,128)(2,1)} %all-gather.6.cloned.1.call-done) | copy-start | bytes 9437188
  195.4 4.3 %copy-start.16 = (f32[512,512]{1,0:T(8,128)S(1)}, f32[512,512]{1,0:T(8,128)}, u32[]{:S(2)}) copy-start(f32[512,512]{1,0:T(8,128)} %copy-done.15) | copy-start | bytes 3145732
  199.7 4.9 %copy-start.1 = (f32[512,512]{1,0:T(8,128)}, f32[512,512]{1,0:T(8,128)S(1)}, u32[]{:S(2)}) copy-start(f32[512,512]{1,0:T(8,128)S(1)} %fusion.22) | copy-start | bytes 3145732
  199.7 2.8 copy-start.3
  208.2 121.8 %all-gather.8.cloned.1.call-start = ((), (), s32[]{:S(2)}) async-start(), calls=%async_computation.6 | async-start | bytes 3342336 | tf_op jit(solution)/shard_map/all_gather | solution.py:40
  208.3 67.3 %collective-permute-start.2 = (bf16[4,32,8]{1,2,0:T(8,128)(2,1)}, bf16[4,32,8]{1,2,0:T(8,128)(2,1)}, u32[]{:S(2)}, u32[]{:S(2)}) collective-permute-start(bf16[4,32,8]{1,2,0:T(8,128)(2,1)} %copy-done.8), channel_id=1, source_target_pairs={{0,16},{1,17},{2,18},{3,19},{4,20},{5,21},{6,22},{7,23},{8,24},{9,... | collective-permute-start | bytes 6152 | tf_op jit(solution)/shard_map/ppermute | solution.py:62
  278.1 7.8 %collective-permute-start.3 = (bf16[4,8,3072]{2,1,0:T(8,128)(2,1)}, bf16[4,8,3072]{2,1,0:T(8,128)(2,1)S(1)}, u32[]{:S(2)}, u32[]{:S(2)}) collective-permute-start(bf16[4,8,3072]{2,1,0:T(8,128)(2,1)} %convolution_convert_fusion.8), channel_id=1, source_target_pairs={{16,0},{17,1},{18,2},{19,3},{20,4},{21,5},{22,6},{23,7},{24,8},{25... | collective-permute-start | bytes 589832 | tf_op jit(solution)/shard_map/ppermute | solution.py:135
  330.0 4.8 %copy-start.2 = (f32[512,512]{1,0:T(8,128)S(1)}, f32[512,512]{1,0:T(8,128)}, u32[]{:S(2)}) copy-start(f32[512,512]{1,0:T(8,128)} %copy-done.1) | copy-start | bytes 3145732
  330.0 4.8 %copy-start.6 = (f32[512,512]{1,0:T(8,128)S(1)}, f32[512,512]{1,0:T(8,128)}, u32[]{:S(2)}) copy-start(f32[512,512]{1,0:T(8,128)} %copy-done.5) | copy-start | bytes 3145732
  330.0 4.8 %copy-start.11 = (bf16[512,3072]{1,0:T(8,128)(2,1)S(1)}, bf16[512,3072]{1,0:T(8,128)(2,1)}, u32[]{:S(2)}) copy-start(bf16[512,3072]{1,0:T(8,128)(2,1)} %all-gather.4.cloned.1.call-done) | copy-start | bytes 9437188
  330.0 5.3 %copy-start.14 = (bf16[512,3072]{1,0:T(8,128)(2,1)S(1)}, bf16[512,3072]{1,0:T(8,128)(2,1)}, u32[]{:S(2)}) copy-start(bf16[512,3072]{1,0:T(8,128)(2,1)} %all-gather.8.cloned.1.call-done) | copy-start | bytes 9437188
  335.3 3.7 %copy-start.13 = (bf16[512,3072]{1,0:T(8,128)(2,1)S(1)}, bf16[512,3072]{1,0:T(8,128)(2,1)}, u32[]{:S(2)}) copy-start(bf16[512,3072]{1,0:T(8,128)(2,1)} %all-gather.6.cloned.1.call-done) | copy-start | bytes 9437188
  (3 other events, 2.2 us)
Sparse Core Ops, SparseCore 0:
  15.1 47.8 all-gather.3
  74.3 65.0 reduce-scatter.2
  150.3 44.9 all-gather.5
  208.3 64.7 reduce-scatter.4
  286.8 43.1 all-gather.7

commit v2 on v1

--- a/solution.py
+++ b/solution.py
@@ -1,6 +1,8 @@
 import jax
 import jax.numpy as jnp
 from jax import lax
+from jax.experimental import pallas as pl
+from jax.experimental.pallas import tpu as pltpu
 from jax.sharding import PartitionSpec as P
 
 CAP = 8
@@ -35,13 +37,282 @@
     return lax.rsqrt(jnp.mean(rows_f * rows_f, axis=-1, keepdims=True) + EPSILON)
 
 
+SIDE = 4
+
+
+def neighbours():
+    e, z = lax.axis_index("expert"), lax.axis_index("dp")
+    mate = e + 1 - 2 * lax.rem(e, 2)
+    across = lax.rem(e + 2, SIDE)
+    return e, z, mate, across
+
+
+def remote(src, dst, send_sem, recv_sem, target):
+    return pltpu.make_async_remote_copy(
+        src_ref=src,
+        dst_ref=dst,
+        send_sem=send_sem,
+        recv_sem=recv_sem,
+        device_id=target,
+        device_id_type=pl.DeviceIdType.MESH,
+    )
+
+
+def entry_barrier(z, mate, across):
+    barrier = pltpu.get_barrier_semaphore()
+
+    def greet(target):
+        pl.semaphore_signal(
+            barrier, inc=1, device_id=target, device_id_type=pl.DeviceIdType.MESH
+        )
+
+    greet({"expert": mate})
+    greet({"expert": across})
+
+    @pl.when(z > 0)
+    def _():
+        greet({"dp": z - 1})
+
+    @pl.when(z < SIDE - 1)
+    def _():
+        greet({"dp": z + 1})
+
+    @pl.when((z > 0) & (z < SIDE - 1))
+    def _():
+        pl.semaphore_wait(barrier, 4)
+
+    @pl.when((z == 0) | (z == SIDE - 1))
+    def _():
+        pl.semaphore_wait(barrier, 3)
+
+
+def gather_kernel(x_ref, out_ref, local_sem, send_sem, recv_sem):
+    e, z, mate, across = neighbours()
+    entry_barrier(z, mate, across)
+
+    def route(slot, kind, target, src=None):
+        block = out_ref.at[slot] if src is None else src
+        return remote(
+            block, out_ref.at[slot], send_sem.at[slot, kind], recv_sem.at[slot], target
+        )
+
+    def up(slot, src=None):
+        return route(slot, 0, {"dp": z + 1}, src)
+
+    def down(slot, src=None):
+        return route(slot, 1, {"dp": z - 1}, src)
+
+    def over(slot, src=None):
+        return route(slot, 2, {"expert": across}, src)
+
+    def core(slot, src=None):
+        return route(slot, 3, {"expert": mate}, src)
+
+    mine = e * SIDE + z
+
+    def own_sends(act):
+        @pl.when(z < SIDE - 1)
+        def _():
+            act(up(mine, x_ref))
+
+        @pl.when(z > 0)
+        def _():
+            act(down(mine, x_ref))
+
+        act(over(mine, x_ref))
+        act(core(mine, x_ref))
+
+    keep = pltpu.make_async_copy(x_ref, out_ref.at[mine], local_sem)
+    own_sends(lambda copy: copy.start())
+    keep.start()
+
+    def chain(act, arrive):
+        for d in range(1, SIDE):
+
+            @pl.when(z - d >= 0)
+            def _():
+                slot = e * SIDE + z - d
+                if arrive:
+                    core(slot).wait_recv()
+
+                @pl.when(z < SIDE - 1)
+                def _():
+                    act(up(slot))
+
+                act(over(slot))
+                act(core(slot))
+
+            @pl.when(z + d < SIDE)
+            def _():
+                slot = e * SIDE + z + d
+                if arrive:
+                    core(slot).wait_recv()
+
+                @pl.when(z > 0)
+                def _():
+                    act(down(slot))
+
+                act(over(slot))
+                act(core(slot))
+
+    chain(lambda copy: copy.start(), True)
+    for d in range(SIDE):
+        slot = across * SIDE + lax.rem(z + d, SIDE)
+        core(slot).wait_recv()
+        core(slot).start()
+    far = lax.rem(mate + 2, SIDE)
+    for d in range(SIDE):
+        core(mate * SIDE + lax.rem(z + d, SIDE)).wait_recv()
+        core(far * SIDE + lax.rem(z + d, SIDE)).wait_recv()
+    own_sends(lambda copy: copy.wait_send())
+    keep.wait()
+    chain(lambda copy: copy.wait_send(), False)
+    for d in range(SIDE):
+        core(across * SIDE + lax.rem(z + d, SIDE)).wait_send()
+
+
+def scatter_kernel(
+    x_ref, out_ref, core_in, over_in, up_in, down_in, over_out, chain_out,
+    core_s, core_r, over_s, over_r, up_s, up_r, down_s, down_r,
+):
+    e, z, mate, across = neighbours()
+    far = lax.rem(mate + 2, SIDE)
+    entry_barrier(z, mate, across)
+    order = [lax.rem(z + d, SIDE) for d in (2, 3, 1, 0)]
+
+    def f32(block):
+        return block.astype(jnp.float32)
+
+    def core(half, q):
+        owner = far if half == 0 else mate
+        return remote(
+            x_ref.at[owner * SIDE + q], core_in.at[half * SIDE + q],
+            core_s.at[half * SIDE + q], core_r.at[half * SIDE + q], {"expert": mate},
+        )
+
+    def over(q):
+        return remote(
+            over_out.at[q], over_in.at[q], over_s.at[q], over_r.at[q], {"expert": across}
+        )
+
+    def up(q):
+        return remote(chain_out.at[q], up_in.at[q], up_s.at[q], up_r.at[q], {"dp": z + 1})
+
+    def down(q):
+        return remote(
+            chain_out.at[q], down_in.at[q], down_s.at[q], down_r.at[q], {"dp": z - 1}
+        )
+
+    for half in range(2):
+        for q in order:
+            core(half, q).start()
+    for q in order:
+        core(0, q).wait_recv()
+        both = f32(x_ref[across * SIDE + q]) + f32(core_in[q])
+        over_out[q] = both.astype(jnp.bfloat16)
+        over(q).start()
+    for q in order[:-1]:
+        core(1, q).wait_recv()
+        over(q).wait_recv()
+        both = f32(x_ref[e * SIDE + q]) + f32(core_in[SIDE + q]) + f32(over_in[q])
+        chain_out[q] = both.astype(jnp.bfloat16)
+
+        @pl.when(q > z)
+        def _():
+            @pl.when(z > 0)
+            def _():
+                up(q).wait_recv()
+                chain_out[q] = (f32(chain_out[q]) + f32(up_in[q])).astype(jnp.bfloat16)
+
+            up(q).start()
+
+        @pl.when(q < z)
+        def _():
+            @pl.when(z < SIDE - 1)
+            def _():
+                down(q).wait_recv()
+                chain_out[q] = (f32(chain_out[q]) + f32(down_in[q])).astype(jnp.bfloat16)
+
+            down(q).start()
+
+    core(1, z).wait_recv()
+    over(z).wait_recv()
+    total = f32(x_ref[e * SIDE + z]) + f32(core_in[SIDE + z]) + f32(over_in[z])
+
+    @pl.when(z == 0)
+    def _():
+        down(z).wait_recv()
+        out_ref[...] = (total + f32(down_in[z])).astype(jnp.bfloat16)
+
+    @pl.when(z == SIDE - 1)
+    def _():
+        up(z).wait_recv()
+        out_ref[...] = (total + f32(up_in[z])).astype(jnp.bfloat16)
+
+    @pl.when((z > 0) & (z < SIDE - 1))
+    def _():
+        up(z).wait_recv()
+        down(z).wait_recv()
+        out_ref[...] = (total + f32(up_in[z]) + f32(down_in[z])).astype(jnp.bfloat16)
+
+    for half in range(2):
+        for q in order:
+            core(half, q).wait_send()
+    for q in order:
+        over(q).wait_send()
+    for q in order[:-1]:
+
+        @pl.when(q > z)
+        def _():
+            up(q).wait_send()
+
+        @pl.when(q < z)
+        def _():
+            down(q).wait_send()
+
+
+def square_group():
+    return lax.axis_size("expert") == SIDE and lax.axis_size("dp") == SIDE
+
+
 def gather(block):
     flat = block.reshape(-1, block.shape[-1])
-    return lax.all_gather(flat, GROUP, axis=0, tiled=True)
+    if not square_group():
+        return lax.all_gather(flat, GROUP, axis=0, tiled=True)
+    slots = SIDE * SIDE
+    got = pl.pallas_call(
+        gather_kernel,
+        out_shape=jax.ShapeDtypeStruct((slots,) + flat.shape, flat.dtype),
+        in_specs=[pl.BlockSpec(memory_space=pl.ANY)],
+        out_specs=pl.BlockSpec(memory_space=pl.ANY),
+        scratch_shapes=[
+            pltpu.SemaphoreType.DMA,
+            pltpu.SemaphoreType.DMA((slots, 4)),
+            pltpu.SemaphoreType.DMA((slots,)),
+        ],
+        compiler_params=pltpu.CompilerParams(collective_id=0, has_side_effects=True),
+    )(flat)
+    return got.reshape(-1, flat.shape[-1])
 
 
 def scatter_sum(partial, like):
-    summed = lax.psum_scatter(partial, GROUP, scatter_dimension=0, tiled=True)
+    if not square_group():
+        summed = lax.psum_scatter(partial, GROUP, scatter_dimension=0, tiled=True)
+        return summed.reshape(like.shape)
+    width = partial.shape[-1]
+    rows = partial.shape[0] // (SIDE * SIDE)
+    buffers = [pltpu.VMEM((n, rows, width), partial.dtype) for n in (8, 4, 4, 4, 4, 4)]
+    sems = [pltpu.SemaphoreType.DMA((n,)) for n in (8, 8, 4, 4, 4, 4, 4, 4)]
+    summed = pl.pallas_call(
+        scatter_kernel,
+        out_shape=jax.ShapeDtypeStruct((rows, width), partial.dtype),
+        in_specs=[pl.BlockSpec(memory_space=pltpu.VMEM)],
+        out_specs=pl.BlockSpec(memory_space=pltpu.VMEM),
+        scratch_shapes=buffers + sems,
+        compiler_params=pltpu.CompilerParams(
+            collective_id=1, has_side_effects=True, vmem_limit_bytes=32 * 1024 * 1024
+        ),
+    )(partial.reshape(SIDE * SIDE, rows, width))
     return summed.reshape(like.shape)
 
 

time: 354 us -> 231 us (0.65)
  waiting for transfers between devices: 265 us -> 6.27 us
  Pallas kernels: 0 us -> 148 us
  between operations: 14 us -> 0.98 us
  matrix products: 52 us -> 44.7 us
    pallas_call x0 -> x5, Pallas kernels: none -> 148 us  [the longest x3 79.9 us: gather(): pl.pallas_call(gather_kernel, out_shape=jax.ShapeDtypeStruct((slots,) + f...]
    all_gather x3 -> x0, waiting for transfers between devices: 131 us -> none  [gather(): return lax.all_gather(flat, GROUP, axis=0, tiled=True)]
    reduce_scatter x2 -> x0, waiting for transfers between devices: 120 us -> none  [scatter_sum(): summed = lax.psum_scatter(partial, GROUP, scatter_dimension=0, tiled=True)]
    dot_general x12, matrix products: 43.4 us -> 37 us  [mm(): lax.dot_general(a, b, (dims, ((), ())), preferred_element_type=jnp.float32)]
    ppermute x1, waiting for transfers between devices: 4.35 us -> 0.01 us  [shards(): next_table = lax.ppermute(table, 'section', down_route)]
    select_n x0 -> x2, other arithmetic: none -> 3.64 us  [shards(): all_grads = jnp.where(active, got, all_grads)]
  transfers between devices with their start and end apart: 9 -> 4, of which waited for: 8 -> 1; matrix products, arithmetic and copies ran while one was open for 2% -> 15% of each run, Pallas kernels for 0% -> 53%
where the time goes in v2:
time: 231 us
  Pallas kernels  148 us (64%)
  matrix products  44.7 us (19%)
  starting transfers between devices  13 us (6%)
  other arithmetic  11.8 us (5%)
  waiting for transfers between devices  6.27 us (3%)
  local copies, waits for them, and re-layouts  5.8 us (3%)
    pallas_call x3, Pallas kernels, gather(): pl.pallas_call(gather_kernel, out_shape=jax.ShapeDtypeStruct((slots,) + f...  79.9 us
    pallas_call x2, Pallas kernels, scatter_sum(): pl.pallas_call(scatter_kernel, out_shape=jax.ShapeDtypeStruct((rows, widt...  68.1 us
    dot_general x12, matrix products, mm(): lax.dot_general(a, b, (dims, ((), ())), preferred_element_type=jnp.float32)  37 us
    dot_general x4, matrix products, pick(): lax.dot_general(table, values, (((1,), (1,)), ((0,), (0,))), preferred_el...  7.68 us
    ppermute x1, waiting for transfers between devices, shards(): grads_in = lax.ppermute(pick(previous_table, result), 'section', down_route)  6.26 us
    unnamed x42, local copies, waits for them, and re-layouts  5.8 us
    ppermute x1, starting transfers between devices, shards(): previous_table = lax.ppermute(table, 'section', up_route)  5.43 us
    ppermute x1, starting transfers between devices, shards(): current = lax.ppermute(pick(next_table, output), 'section', up_route)  5.01 us
  transfers between devices with their start and end apart: 4, of which 1 were waited for; matrix products, arithmetic and copies ran while one was open for 15% of the time, Pallas kernels for 53%

profile of v2, /device:TPU:0, one launch (start us, length us, event | category | flops | bytes accessed | tf_op | source)
XLA Modules:
  0.0 230.6 jit_solution(11562688076289932283)
XLA Ops:
  3.1 5.4 %collective-permute-start.2 = (bf16[4,32,8]{1,2,0:T(8,128)(2,1)}, bf16[4,32,8]{1,2,0:T(8,128)(2,1)}, u32[]{:S(2)}, u32[]{:S(2)}) collective-permute-start(bf16[4,32,8]{1,2,0:T(8,128)(2,1)} %fusion.70), channel_id=1, source_target_pairs={{0,16},{1,17},{2,18},{3,19},{4,20},{5,21},{6,22},{7,23},{8,24},{9,... | collective-permute-start | bytes 6152 | tf_op jit(solution)/shard_map/ppermute | solution.py:333
  10.6 2.0 fusion.37
  14.0 1.9 fusion.44.x_ref
  15.9 27.3 %shard_map.94 = bf16[16,32,3072]{2,1,0:T(8,128)(2,1)} custom-call(bf16[32,3072]{1,0:T(8,128)(2,1)} %fusion.44.x_ref), custom_call_target="tpu_custom_call" | custom-call | tf_op jit(solution)/shard_map/pallas_call | solution.py:283
  43.2 4.8 %fusion.14 = f32[512,512]{1,0:T(8,128)S(1)} fusion(bf16[512,3072]{1,0:T(8,128)(2,1)} %bitcast.76, bf16[1,3072,512]{2,1,0:T(8,128)(2,1)} %param.12), kind=kOutput, calls=%fused_computation.26 | convolution fusion | flops 1610612736 | bytes 7340032 | tf_op jit(solution)/shard_map/dot_general | solution.py:320
  48.0 1.8 fusion.20
  50.3 1.8 convolution_convert_fusion.3
  52.1 33.6 %shard_map.95 = bf16[32,3072]{1,0:T(8,128)(2,1)S(1)} custom-call(bf16[16,32,3072]{2,1,0:T(8,128)(2,1)S(1)} %bitcast.75), custom_call_target="tpu_custom_call" | custom-call | tf_op jit(solution)/shard_map/pallas_call | solution.py:306
  85.8 2.4 %convolution_convert_fusion.9 = bf16[4,8,3072]{2,1,0:T(8,128)(2,1)} fusion(bf16[4,32,8]{1,2,0:T(8,128)(2,1)} %collective-permute-done, bf16[4,32,3072]{2,1,0:T(8,128)(2,1)} %param.7, pred[4,32]{1,0:T(4,128)(4,1)S(1)} %broadcast_compare_fusion, bf16[4,8,3072]{2,1,0:T(8,128)(2,1)S(1)} %copy-done.13, bf16[32,3072]{1,0:T(8,128)(2,1)S(1)} %shard_map.95, ...), kind=kOutput, calls=%fused_computation.16 | convolution fusion | flops 13961216 | bytes 1379072 | tf_op jit(solution)/shard_map/dot_general | solution.py:24
  88.2 5.0 %collective-permute-start.1 = (bf16[4,8,3072]{2,1,0:T(8,128)(2,1)}, bf16[4,8,3072]{2,1,0:T(8,128)(2,1)S(1)}, u32[]{:S(2)}, u32[]{:S(2)}) collective-permute-start(bf16[4,8,3072]{2,1,0:T(8,128)(2,1)} %convolution_convert_fusion.9), channel_id=1, source_target_pairs={{0,16},{1,17},{2,18},{3,19},{4,20},{5,21},{6,22},{7,23},{8,24},{9,... | collective-permute-start | bytes 589832 | tf_op jit(solution)/shard_map/ppermute | solution.py:374
  93.2 5.6 %fusion.8 = f32[512,512]{1,0:T(8,128)} fusion(bf16[512,3072]{1,0:T(8,128)(2,1)} %bitcast.77, bf16[1,512,3072]{2,1,0:T(8,128)(2,1)} %param.13), kind=kOutput, calls=%fused_computation.20 | convolution fusion | flops 1610612736 | bytes 7340032 | tf_op jit(solution)/shard_map/dot_general | solution.py:320
  100.3 25.9 %shard_map.96 = bf16[16,32,3072]{2,1,0:T(8,128)(2,1)} custom-call(bf16[32,3072]{1,0:T(8,128)(2,1)} %fusion.50.x_ref), custom_call_target="tpu_custom_call" | custom-call | tf_op jit(solution)/shard_map/pallas_call | solution.py:283
  126.2 4.1 %fusion.22 = f32[512,512]{1,0:T(8,128)S(1)} fusion(f32[512,512]{1,0:T(8,128)} %copy-done.20, bf16[512,3072]{1,0:T(8,128)(2,1)} %bitcast.81, bf16[1,3072,512]{2,1,0:T(8,128)(2,1)S(1)} %copy-done, pred[]{:T(512)S(6)} %eq.31), kind=kOutput, calls=%fused_computation.36 | convolution fusion | flops 1610874880 | bytes 8388609 | tf_op jit(solution)/shard_map/dot_general | solution.py:320
  133.3 2.1 fusion.16
  135.4 1.9 add_convert_fusion
  137.3 34.5 %shard_map.97 = bf16[32,3072]{1,0:T(8,128)(2,1)S(1)} custom-call(bf16[16,32,3072]{2,1,0:T(8,128)(2,1)S(1)} %bitcast.74), custom_call_target="tpu_custom_call" | custom-call | tf_op jit(solution)/shard_map/pallas_call | solution.py:306
  173.2 1.9 convolution_convert_fusion.8
  176.5 6.3 %collective-permute-done.3 = bf16[4,8,3072]{2,1,0:T(8,128)(2,1)S(1)} collective-permute-done((bf16[4,8,3072]{2,1,0:T(8,128)(2,1)S(1)}, bf16[4,8,3072]{2,1,0:T(8,128)(2,1)S(1)}, u32[]{:S(2)}, u32[]{:S(2)}) %collective-permute-start.3) | collective-permute-done | bytes 196640 | tf_op jit(solution)/shard_map/ppermute | solution.py:406
  183.5 26.7 %shard_map.98 = bf16[16,32,3072]{2,1,0:T(8,128)(2,1)} custom-call(bf16[32,3072]{1,0:T(8,128)(2,1)} %fusion.45.x_ref), custom_call_target="tpu_custom_call" | custom-call | tf_op jit(solution)/shard_map/pallas_call | solution.py:283
  210.2 3.3 %bitcast_select_fusion = bf16[512,3072]{1,0:T(8,128)(2,1)S(1)} fusion(bf16[16,32,3072]{2,1,0:T(8,128)(2,1)} %shard_map.98, pred[]{:T(512)S(6)} %eq.36, bf16[16,32,3072]{2,1,0:T(8,128)(2,1)} %shard_map.94), kind=kLoop, calls=%fused_computation.17 | loop fusion | flops 1572864 | bytes 9437185 | tf_op jit(solution)/shard_map/jit(_where)/select_n | solution.py:391
  216.8 1.8 fusion.6
  219.3 3.8 %fusion = bf16[1,3072,512]{2,1,0:T(8,128)(2,1)} fusion(bf16[512,3072]{1,0:T(8,128)(2,1)S(1)} %bitcast.83, bf16[512,3072]{1,0:T(8,128)(2,1)S(1)} %bitcast.79, pred[]{:T(512)S(6)} %eq.31, f32[512,512]{1,0:T(8,128)S(1)} %fusion.6, f32[512,512]{1,0:T(8,128)S(1)} %copy-done.5, f32[512,512]{1,0:T(8,128)S(1)} %copy-done.8), kind=kOutput, calls=%fused_computation.5 | convolution fusion | flops 1616379904 | bytes 12582913 | tf_op jit(solution)/shard_map/dot_general | solution.py:320
  223.1 3.8 %fusion.1 = bf16[1,3072,512]{2,1,0:T(8,128)(2,1)} fusion(bf16[512,3072]{1,0:T(8,128)(2,1)S(1)} %bitcast.84, bf16[512,3072]{1,0:T(8,128)(2,1)S(1)} %bitcast.80, pred[]{:T(512)S(6)} %eq.31, f32[512,512]{1,0:T(8,128)S(1)} %fusion.6, f32[512,512]{1,0:T(8,128)S(1)} %copy-done.5), kind=kOutput, calls=%fused_computation.6 | convolution fusion | flops 1615331328 | bytes 11534337 | tf_op jit(solution)/shard_map/dot_general | solution.py:320
  226.9 3.6 %fusion.2 = bf16[1,512,3072]{2,1,0:T(8,128)(2,1)} fusion(bf16[512,3072]{1,0:T(8,128)(2,1)S(1)} %bitcast_select_fusion, f32[512,512]{1,0:T(8,128)S(1)} %copy-done.8, f32[512,512]{1,0:T(8,128)S(1)} %copy-done.5), kind=kOutput, calls=%fused_computation.7 | convolution fusion | flops 1613758464 | bytes 8388608 | tf_op jit(solution)/shard_map/dot_general | solution.py:320
  (62 shorter events, 18.2 us)
Async XLA Ops:
  0.6 47.4 %copy-start = (bf16[1,3072,512]{2,1,0:T(8,128)(2,1)S(1)}, bf16[1,3072,512]{2,1,0:T(8,128)(2,1)}, u32[]{:S(2)}) copy-start(bf16[1,3072,512]{2,1,0:T(8,128)(2,1)} %param.11) | copy-start | bytes 9437188
  3.1 170.2 %collective-permute-start.2 = (bf16[4,32,8]{1,2,0:T(8,128)(2,1)}, bf16[4,32,8]{1,2,0:T(8,128)(2,1)}, u32[]{:S(2)}, u32[]{:S(2)}) collective-permute-start(bf16[4,32,8]{1,2,0:T(8,128)(2,1)} %fusion.70), channel_id=1, source_target_pairs={{0,16},{1,17},{2,18},{3,19},{4,20},{5,21},{6,22},{7,23},{8,24},{9,... | collective-permute-start | bytes 6152 | tf_op jit(solution)/shard_map/ppermute | solution.py:333
  8.5 77.3 %collective-permute-start = (bf16[4,32,8]{1,2,0:T(8,128)(2,1)}, bf16[4,32,8]{1,2,0:T(8,128)(2,1)}, u32[]{:S(2)}, u32[]{:S(2)}) collective-permute-start(bf16[4,32,8]{1,2,0:T(8,128)(2,1)} %fusion.70), channel_id=1, source_target_pairs={{16,0},{17,1},{18,2},{19,3},{20,4},{21,5},{22,6},{23,7},{24,8},{25... | collective-permute-start | bytes 6152 | tf_op jit(solution)/shard_map/ppermute | solution.py:332
  14.0 34.0 %copy-start.9 = (f32[4,8,3072]{2,1,0:T(8,128)}, f32[4,8,3072]{2,1,0:T(8,128)S(1)}, u32[]{:S(2)}) copy-start(f32[4,8,3072]{2,1,0:T(8,128)S(1)} %fusion.5) | copy-start | bytes 1179652
  43.2 4.8 %copy-start.1 = (bf16[16,32,3072]{2,1,0:T(8,128)(2,1)S(1)}, bf16[16,32,3072]{2,1,0:T(8,128)(2,1)}, u32[]{:S(2)}) copy-start(bf16[16,32,3072]{2,1,0:T(8,128)(2,1)} %shard_map.94) | copy-start | bytes 9437188
  48.0 1.8 copy-start.18
  48.0 2.3 copy-start.16
  50.3 1.8 copy-start.20
  52.1 33.7 %copy-start.13 = (bf16[4,8,3072]{2,1,0:T(8,128)(2,1)S(1)}, bf16[4,8,3072]{2,1,0:T(8,128)(2,1)}, u32[]{:S(2)}) copy-start(bf16[4,8,3072]{2,1,0:T(8,128)(2,1)} %get-tuple-element.9) | copy-start | bytes 589828
  88.2 10.7 %collective-permute-start.1 = (bf16[4,8,3072]{2,1,0:T(8,128)(2,1)}, bf16[4,8,3072]{2,1,0:T(8,128)(2,1)S(1)}, u32[]{:S(2)}, u32[]{:S(2)}) collective-permute-start(bf16[4,8,3072]{2,1,0:T(8,128)(2,1)} %convolution_convert_fusion.9), channel_id=1, source_target_pairs={{0,16},{1,17},{2,18},{3,19},{4,20},{5,21},{6,22},{7,23},{8,24},{9,... | collective-permute-start | bytes 589832 | tf_op jit(solution)/shard_map/ppermute | solution.py:374
  126.2 4.1 %copy-start.10 = (bf16[1,3072,512]{2,1,0:T(8,128)(2,1)S(1)}, bf16[1,3072,512]{2,1,0:T(8,128)(2,1)}, u32[]{:S(2)}) copy-start(bf16[1,3072,512]{2,1,0:T(8,128)(2,1)} %param.12) | copy-start | bytes 9437188
  126.2 4.1 %copy-start.11 = (bf16[16,32,3072]{2,1,0:T(8,128)(2,1)S(1)}, bf16[16,32,3072]{2,1,0:T(8,128)(2,1)}, u32[]{:S(2)}) copy-start(bf16[16,32,3072]{2,1,0:T(8,128)(2,1)} %shard_map.96) | copy-start | bytes 9437188
  126.2 4.3 %copy-start.19 = (f32[512,512]{1,0:T(8,128)S(1)}, f32[512,512]{1,0:T(8,128)}, u32[]{:S(2)}) copy-start(f32[512,512]{1,0:T(8,128)} %copy-done.18) | copy-start | bytes 3145732
  130.5 4.9 %copy-start.4 = (f32[512,512]{1,0:T(8,128)}, f32[512,512]{1,0:T(8,128)S(1)}, u32[]{:S(2)}) copy-start(f32[512,512]{1,0:T(8,128)S(1)} %fusion.22) | copy-start | bytes 3145732
  130.5 2.8 %copy-start.6 = (f32[512,512]{1,0:T(8,128)S(1)}, f32[512,512]{1,0:T(8,128)}, u32[]{:S(2)}) copy-start(f32[512,512]{1,0:T(8,128)} %fusion.8) | copy-start | bytes 3145732
  132.3 1.0 copy-start.7
  137.3 34.5 %copy-start.15 = (bf16[4,8,3072]{2,1,0:T(8,128)(2,1)S(1)}, bf16[4,8,3072]{2,1,0:T(8,128)(2,1)}, u32[]{:S(2)}) copy-start(bf16[4,8,3072]{2,1,0:T(8,128)(2,1)} %copy-done.14) | copy-start | bytes 589828
  175.2 7.6 %collective-permute-start.3 = (bf16[4,8,3072]{2,1,0:T(8,128)(2,1)S(1)}, bf16[4,8,3072]{2,1,0:T(8,128)(2,1)S(1)}, u32[]{:S(2)}, u32[]{:S(2)}) collective-permute-start(bf16[4,8,3072]{2,1,0:T(8,128)(2,1)S(1)} %convolution_convert_fusion.8), channel_id=1, source_target_pairs={{16,0},{17,1},{18,2},{19,3},{20,4},{21,5},{22,6},{23,7},{24,8},{25... | collective-permute-start | bytes 589832 | tf_op jit(solution)/shard_map/ppermute | solution.py:406
  210.2 3.7 %copy-start.2 = (bf16[16,32,3072]{2,1,0:T(8,128)(2,1)S(1)}, bf16[16,32,3072]{2,1,0:T(8,128)(2,1)}, u32[]{:S(2)}) copy-start(bf16[16,32,3072]{2,1,0:T(8,128)(2,1)} %shard_map.94) | copy-start | bytes 9437188
  210.2 4.7 %copy-start.3 = (bf16[16,32,3072]{2,1,0:T(8,128)(2,1)S(1)}, bf16[16,32,3072]{2,1,0:T(8,128)(2,1)}, u32[]{:S(2)}) copy-start(bf16[16,32,3072]{2,1,0:T(8,128)(2,1)} %shard_map.98) | copy-start | bytes 9437188
  214.9 1.9 copy-start.17
  216.8 1.8 copy-start.5
  216.8 1.8 copy-start.8
  216.8 2.5 %copy-start.12 = (bf16[16,32,3072]{2,1,0:T(8,128)(2,1)S(1)}, bf16[16,32,3072]{2,1,0:T(8,128)(2,1)}, u32[]{:S(2)}) copy-start(bf16[16,32,3072]{2,1,0:T(8,128)(2,1)} %shard_map.96) | copy-start | bytes 9437188
  (1 other events, 0.7 us)

commit v3 on v1

--- a/solution.py
+++ b/solution.py
@@ -1,6 +1,8 @@
 import jax
 import jax.numpy as jnp
 from jax import lax
+from jax.experimental import pallas as pl
+from jax.experimental.pallas import tpu as pltpu
 from jax.sharding import PartitionSpec as P
 
 CAP = 8
@@ -35,13 +37,308 @@
     return lax.rsqrt(jnp.mean(rows_f * rows_f, axis=-1, keepdims=True) + EPSILON)
 
 
+SIDE = 4
+CHUNKS = 2
+
+
+def neighbours():
+    e, z = lax.axis_index("expert"), lax.axis_index("dp")
+    mate = e + 1 - 2 * lax.rem(e, 2)
+    across = lax.rem(e + 2, SIDE)
+    return e, z, mate, across
+
+
+def remote(src, dst, send_sem, recv_sem, target):
+    return pltpu.make_async_remote_copy(
+        src_ref=src,
+        dst_ref=dst,
+        send_sem=send_sem,
+        recv_sem=recv_sem,
+        device_id=target,
+        device_id_type=pl.DeviceIdType.MESH,
+    )
+
+
+def entry_barrier(z, mate, across):
+    barrier = pltpu.get_barrier_semaphore()
+
+    def greet(target):
+        pl.semaphore_signal(
+            barrier, inc=1, device_id=target, device_id_type=pl.DeviceIdType.MESH
+        )
+
+    greet({"expert": mate})
+    greet({"expert": across})
+
+    @pl.when(z > 0)
+    def _():
+        greet({"dp": z - 1})
+
+    @pl.when(z < SIDE - 1)
+    def _():
+        greet({"dp": z + 1})
+
+    @pl.when((z > 0) & (z < SIDE - 1))
+    def _():
+        pl.semaphore_wait(barrier, 4)
+
+    @pl.when((z == 0) | (z == SIDE - 1))
+    def _():
+        pl.semaphore_wait(barrier, 3)
+
+
+def gather_kernel(x_ref, out_ref, local_sem, send_sem, recv_sem):
+    e, z, mate, across = neighbours()
+    entry_barrier(z, mate, across)
+
+    def route(h, slot, kind, target, mine=False):
+        block = x_ref.at[h] if mine else out_ref.at[h, slot]
+        return remote(
+            block, out_ref.at[h, slot], send_sem.at[h, slot, kind], recv_sem.at[h, slot], target
+        )
+
+    def up(h, slot, mine=False):
+        return route(h, slot, 0, {"dp": z + 1}, mine)
+
+    def down(h, slot, mine=False):
+        return route(h, slot, 1, {"dp": z - 1}, mine)
+
+    def over(h, slot, mine=False):
+        return route(h, slot, 2, {"expert": across}, mine)
+
+    def core(h, slot, mine=False):
+        return route(h, slot, 3, {"expert": mate}, mine)
+
+    own = e * SIDE + z
+
+    def own_sends(act):
+        for h in range(CHUNKS):
+
+            @pl.when(z < SIDE - 1)
+            def _():
+                act(up(h, own, True))
+
+            @pl.when(z > 0)
+            def _():
+                act(down(h, own, True))
+
+            act(over(h, own, True))
+            act(core(h, own, True))
+
+    def keep(h):
+        return pltpu.make_async_copy(x_ref.at[h], out_ref.at[h, own], local_sem.at[h])
+
+    own_sends(lambda copy: copy.start())
+    for h in range(CHUNKS):
+        keep(h).start()
+
+    def chain(act, arrive):
+        for d in range(1, SIDE):
+            for h in range(CHUNKS):
+
+                @pl.when(z - d >= 0)
+                def _():
+                    slot = e * SIDE + z - d
+                    if arrive:
+                        core(h, slot).wait_recv()
+
+                    @pl.when(z < SIDE - 1)
+                    def _():
+                        act(up(h, slot))
+
+                    act(over(h, slot))
+                    act(core(h, slot))
+
+                @pl.when(z + d < SIDE)
+                def _():
+                    slot = e * SIDE + z + d
+                    if arrive:
+                        core(h, slot).wait_recv()
+
+                    @pl.when(z > 0)
+                    def _():
+                        act(down(h, slot))
+
+                    act(over(h, slot))
+                    act(core(h, slot))
+
+    chain(lambda copy: copy.start(), True)
+    for d in range(SIDE):
+        for h in range(CHUNKS):
+            slot = across * SIDE + lax.rem(z + d, SIDE)
+            core(h, slot).wait_recv()
+            core(h, slot).start()
+    far = lax.rem(mate + 2, SIDE)
+    for h in range(CHUNKS):
+        for d in range(SIDE):
+            core(h, mate * SIDE + lax.rem(z + d, SIDE)).wait_recv()
+            core(h, far * SIDE + lax.rem(z + d, SIDE)).wait_recv()
+    own_sends(lambda copy: copy.wait_send())
+    for h in range(CHUNKS):
+        keep(h).wait()
+    chain(lambda copy: copy.wait_send(), False)
+    for h in range(CHUNKS):
+        for d in range(SIDE):
+            core(h, across * SIDE + lax.rem(z + d, SIDE)).wait_send()
+
+
+def scatter_kernel(
+    x_ref, out_ref, core_in, over_in, up_in, down_in, over_out, chain_out,
+    core_s, core_r, over_s, over_r, up_s, up_r, down_s, down_r,
+):
+    e, z, mate, across = neighbours()
+    far = lax.rem(mate + 2, SIDE)
+    entry_barrier(z, mate, across)
+    order = [lax.rem(z + d, SIDE) for d in (2, 3, 1, 0)]
+
+    def f32(block):
+        return block.astype(jnp.float32)
+
+    def core(h, half, q):
+        owner = far if half == 0 else mate
+        return remote(
+            x_ref.at[h, owner * SIDE + q], core_in.at[h, half * SIDE + q],
+            core_s.at[h, half * SIDE + q], core_r.at[h, half * SIDE + q], {"expert": mate},
+        )
+
+    def over(h, q):
+        return remote(
+            over_out.at[h, q], over_in.at[h, q], over_s.at[h, q], over_r.at[h, q],
+            {"expert": across},
+        )
+
+    def up(h, q):
+        return remote(
+            chain_out.at[h, q], up_in.at[h, q], up_s.at[h, q], up_r.at[h, q], {"dp": z + 1}
+        )
+
+    def down(h, q):
+        return remote(
+            chain_out.at[h, q], down_in.at[h, q], down_s.at[h, q], down_r.at[h, q],
+            {"dp": z - 1},
+        )
+
+    def steps(places):
+        return [(q, h) for q in places for h in range(CHUNKS)]
+
+    for half in range(2):
+        for q, h in steps(order):
+            core(h, half, q).start()
+    for q, h in steps(order):
+        core(h, 0, q).wait_recv()
+        both = f32(x_ref[h, across * SIDE + q]) + f32(core_in[h, q])
+        over_out[h, q] = both.astype(jnp.bfloat16)
+        over(h, q).start()
+
+    def here(h, q):
+        core(h, 1, q).wait_recv()
+        over(h, q).wait_recv()
+        return f32(x_ref[h, e * SIDE + q]) + f32(core_in[h, SIDE + q]) + f32(over_in[h, q])
+
+    for q, h in steps(order[:-1]):
+        both = here(h, q)
+
+        @pl.when(((q > z) & (z == 0)) | ((q < z) & (z == SIDE - 1)))
+        def _():
+            chain_out[h, q] = both.astype(jnp.bfloat16)
+
+        @pl.when((q > z) & (z > 0))
+        def _():
+            up(h, q).wait_recv()
+            chain_out[h, q] = (both + f32(up_in[h, q])).astype(jnp.bfloat16)
+
+        @pl.when((q < z) & (z < SIDE - 1))
+        def _():
+            down(h, q).wait_recv()
+            chain_out[h, q] = (both + f32(down_in[h, q])).astype(jnp.bfloat16)
+
+        @pl.when(q > z)
+        def _():
+            up(h, q).start()
+
+        @pl.when(q < z)
+        def _():
+            down(h, q).start()
+
+    for h in range(CHUNKS):
+        total = here(h, z)
+
+        @pl.when(z == 0)
+        def _():
+            down(h, z).wait_recv()
+            out_ref[h] = (total + f32(down_in[h, z])).astype(jnp.bfloat16)
+
+        @pl.when(z == SIDE - 1)
+        def _():
+            up(h, z).wait_recv()
+            out_ref[h] = (total + f32(up_in[h, z])).astype(jnp.bfloat16)
+
+        @pl.when((z > 0) & (z < SIDE - 1))
+        def _():
+            up(h, z).wait_recv()
+            down(h, z).wait_recv()
+            out_ref[h] = (total + f32(up_in[h, z]) + f32(down_in[h, z])).astype(jnp.bfloat16)
+
+    for half in range(2):
+        for q, h in steps(order):
+            core(h, half, q).wait_send()
+    for q, h in steps(order):
+        over(h, q).wait_send()
+    for q, h in steps(order[:-1]):
+
+        @pl.when(q > z)
+        def _():
+            up(h, q).wait_send()
+
+        @pl.when(q < z)
+        def _():
+            down(h, q).wait_send()
+
+
+def square_group():
+    return lax.axis_size("expert") == SIDE and lax.axis_size("dp") == SIDE
+
+
 def gather(block):
     flat = block.reshape(-1, block.shape[-1])
-    return lax.all_gather(flat, GROUP, axis=0, tiled=True)
+    if not square_group():
+        return lax.all_gather(flat, GROUP, axis=0, tiled=True)
+    slots = SIDE * SIDE
+    width = flat.shape[-1]
+    chunk = flat.shape[0] // CHUNKS
+    got = pl.pallas_call(
+        gather_kernel,
+        out_shape=jax.ShapeDtypeStruct((CHUNKS, slots, chunk, width), flat.dtype),
+        in_specs=[pl.BlockSpec(memory_space=pl.ANY)],
+        out_specs=pl.BlockSpec(memory_space=pl.ANY),
+        scratch_shapes=[
+            pltpu.SemaphoreType.DMA((CHUNKS,)),
+            pltpu.SemaphoreType.DMA((CHUNKS, slots, 4)),
+            pltpu.SemaphoreType.DMA((CHUNKS, slots)),
+        ],
+        compiler_params=pltpu.CompilerParams(collective_id=0, has_side_effects=True),
+    )(flat.reshape(CHUNKS, chunk, width))
+    return got.reshape(-1, width)
 
 
 def scatter_sum(partial, like):
-    summed = lax.psum_scatter(partial, GROUP, scatter_dimension=0, tiled=True)
+    if not square_group():
+        summed = lax.psum_scatter(partial, GROUP, scatter_dimension=0, tiled=True)
+        return summed.reshape(like.shape)
+    width = partial.shape[-1]
+    rows = partial.shape[0] // (SIDE * SIDE * CHUNKS)
+    buffers = [pltpu.VMEM((CHUNKS, n, rows, width), partial.dtype) for n in (8, 4, 4, 4, 4, 4)]
+    sems = [pltpu.SemaphoreType.DMA((CHUNKS, n)) for n in (8, 8, 4, 4, 4, 4, 4, 4)]
+    summed = pl.pallas_call(
+        scatter_kernel,
+        out_shape=jax.ShapeDtypeStruct((CHUNKS, rows, width), partial.dtype),
+        in_specs=[pl.BlockSpec(memory_space=pltpu.VMEM)],
+        out_specs=pl.BlockSpec(memory_space=pltpu.VMEM),
+        scratch_shapes=buffers + sems,
+        compiler_params=pltpu.CompilerParams(
+            collective_id=1, has_side_effects=True, vmem_limit_bytes=32 * 1024 * 1024
+        ),
+    )(partial.reshape(CHUNKS, SIDE * SIDE, rows, width))
     return summed.reshape(like.shape)
 
 

time: 354 us -> 215 us (0.61)
  waiting for transfers between devices: 265 us -> 6.27 us
  Pallas kernels: 0 us -> 134 us
  between operations: 14 us -> 0.95 us
  matrix products: 52 us -> 44.9 us
    pallas_call x0 -> x5, Pallas kernels: none -> 134 us  [the longest x3 73.1 us: gather(): pl.pallas_call(gather_kernel, out_shape=jax.ShapeDtypeStruct((CHUNKS, slo...]
    all_gather x3 -> x0, waiting for transfers between devices: 131 us -> none  [gather(): return lax.all_gather(flat, GROUP, axis=0, tiled=True)]
    reduce_scatter x2 -> x0, waiting for transfers between devices: 120 us -> none  [scatter_sum(): summed = lax.psum_scatter(partial, GROUP, scatter_dimension=0, tiled=True)]
    dot_general x12, matrix products: 43.4 us -> 37 us  [mm(): lax.dot_general(a, b, (dims, ((), ())), preferred_element_type=jnp.float32)]
    ppermute x1, waiting for transfers between devices: 4.35 us -> 0.01 us  [shards(): next_table = lax.ppermute(table, 'section', down_route)]
    select_n x0 -> x2, other arithmetic: none -> 3.64 us  [shards(): all_grads = jnp.where(active, got, all_grads)]
  transfers between devices with their start and end apart: 9 -> 4, of which waited for: 8 -> 1; matrix products, arithmetic and copies ran while one was open for 2% -> 15% of each run, Pallas kernels for 0% -> 51%
where the time goes in v3:
time: 215 us; the launch traced here: 214 us
  Pallas kernels  134 us (62%)
  matrix products  44.9 us (21%)
  starting transfers between devices  12.9 us (6%)
  other arithmetic  9.95 us (5%)
  waiting for transfers between devices  6.27 us (3%)
  local copies, waits for them, and re-layouts  5.79 us (3%)
    pallas_call x3, Pallas kernels, gather(): pl.pallas_call(gather_kernel, out_shape=jax.ShapeDtypeStruct((CHUNKS, slo...  73.1 us
    pallas_call x2, Pallas kernels, scatter_sum(): pl.pallas_call(scatter_kernel, out_shape=jax.ShapeDtypeStruct((CHUNKS, ro...  60.6 us
    dot_general x12, matrix products, mm(): lax.dot_general(a, b, (dims, ((), ())), preferred_element_type=jnp.float32)  37 us
    dot_general x4, matrix products, pick(): lax.dot_general(table, values, (((1,), (1,)), ((0,), (0,))), preferred_el...  7.9 us
    ppermute x1, waiting for transfers between devices, shards(): grads_in = lax.ppermute(pick(previous_table, result), 'section', down_route)  6.26 us
    unnamed x38, local copies, waits for them, and re-layouts  5.79 us
    ppermute x1, starting transfers between devices, shards(): previous_table = lax.ppermute(table, 'section', up_route)  5.43 us
    ppermute x1, starting transfers between devices, shards(): current = lax.ppermute(pick(next_table, output), 'section', up_route)  4.94 us
  transfers between devices with their start and end apart: 4, of which 1 were waited for; matrix products, arithmetic and copies ran while one was open for 15% of the time, Pallas kernels for 51%

profile of v3, /device:TPU:0, one launch (start us, length us, event | category | flops | bytes accessed | tf_op | source)
XLA Modules:
  0.0 214.5 jit_solution(12524741788410473425)
XLA Ops:
  3.1 5.4 %collective-permute-start.2 = (bf16[4,32,8]{1,2,0:T(8,128)(2,1)}, bf16[4,32,8]{1,2,0:T(8,128)(2,1)}, u32[]{:S(2)}, u32[]{:S(2)}) collective-permute-start(bf16[4,32,8]{1,2,0:T(8,128)(2,1)} %fusion.63), channel_id=1, source_target_pairs={{0,16},{1,17},{2,18},{3,19},{4,20},{5,21},{6,22},{7,23},{8,24},{9,... | collective-permute-start | bytes 6152 | tf_op jit(solution)/shard_map/ppermute | solution.py:359
  12.0 2.2 %fusion.43 = (bf16[4,8,3072]{2,1,0:T(8,128)(2,1)}, f32[4,8,3072]{2,1,0:T(8,128)}) fusion(bf16[4,8,3072]{2,1,0:T(8,128)(2,1)S(1)} %get-tuple-element.9, f32[4,8]{1,0:T(4,128)S(1)} %add_rsqrt_fusion.2, f32[4,8]{1,0:T(4,128)S(1)} %multiply_reduce_fusion, pred[]{:T(512)S(6)} %eq.31, bf16[4,32,3072]{2,1,0:T(8,128)(2,1)} %param.8, ...), kind=kOutput, calls=%fused_computation.73 | convolution fusion | flops 7079936 | bytes 1573761 | tf_op jit(solution)/shard_map/dot_general | solution.py:24
  14.2 24.9 %shard_map.94 = bf16[2,16,16,3072]{3,2,1,0:T(8,128)(2,1)} custom-call(bf16[2,16,3072]{2,1,0:T(8,128)(2,1)} %bitcast.77), custom_call_target="tpu_custom_call" | custom-call | tf_op jit(solution)/shard_map/pallas_call | solution.py:309
  39.2 4.8 %fusion.14 = f32[512,512]{1,0:T(8,128)S(1)} fusion(bf16[512,3072]{1,0:T(8,128)(2,1)} %bitcast.65, bf16[1,3072,512]{2,1,0:T(8,128)(2,1)} %param.12), kind=kOutput, calls=%fused_computation.26 | convolution fusion | flops 1610612736 | bytes 7340032 | tf_op jit(solution)/shard_map/dot_general | solution.py:346
  44.0 1.8 fusion.20
  46.2 1.8 convolution_convert_fusion.3
  48.1 30.3 %shard_map.95 = bf16[2,16,3072]{2,1,0:T(8,128)(2,1)S(1)} custom-call(bf16[2,16,16,3072]{3,2,1,0:T(8,128)(2,1)S(1)} %bitcast.61), custom_call_target="tpu_custom_call" | custom-call | tf_op jit(solution)/shard_map/pallas_call | solution.py:332
  78.4 2.4 %convolution_convert_fusion.9 = bf16[4,8,3072]{2,1,0:T(8,128)(2,1)} fusion(bf16[4,32,8]{1,2,0:T(8,128)(2,1)} %collective-permute-done, bf16[4,32,3072]{2,1,0:T(8,128)(2,1)} %param.7, pred[4,32]{1,0:T(4,128)(4,1)S(1)} %broadcast_compare_fusion, bf16[4,8,3072]{2,1,0:T(8,128)(2,1)S(1)} %get-tuple-element.9, bf16[4,8,3072]{2,1,0:T(8,128)(2,1)S(1)} %bitcast.64, ...), kind=kOutput, calls=%fused_computation.16 | convolution fusion | flops 13961216 | bytes 1379072 | tf_op jit(solution)/shard_map/dot_general | solution.py:24
  80.8 4.9 %collective-permute-start.1 = (bf16[4,8,3072]{2,1,0:T(8,128)(2,1)}, bf16[4,8,3072]{2,1,0:T(8,128)(2,1)S(1)}, u32[]{:S(2)}, u32[]{:S(2)}) collective-permute-start(bf16[4,8,3072]{2,1,0:T(8,128)(2,1)} %convolution_convert_fusion.9), channel_id=1, source_target_pairs={{0,16},{1,17},{2,18},{3,19},{4,20},{5,21},{6,22},{7,23},{8,24},{9,... | collective-permute-start | bytes 589832 | tf_op jit(solution)/shard_map/ppermute | solution.py:400
  85.7 5.6 %fusion.8 = f32[512,512]{1,0:T(8,128)} fusion(bf16[512,3072]{1,0:T(8,128)(2,1)} %bitcast.66, bf16[1,512,3072]{2,1,0:T(8,128)(2,1)} %param.13), kind=kOutput, calls=%fused_computation.20 | convolution fusion | flops 1610612736 | bytes 7340032 | tf_op jit(solution)/shard_map/dot_general | solution.py:346
  92.8 23.7 %shard_map.96 = bf16[2,16,16,3072]{3,2,1,0:T(8,128)(2,1)} custom-call(bf16[2,16,3072]{2,1,0:T(8,128)(2,1)} %bitcast.76), custom_call_target="tpu_custom_call" | custom-call | tf_op jit(solution)/shard_map/pallas_call | solution.py:309
  116.5 4.1 %fusion.22 = f32[512,512]{1,0:T(8,128)S(1)} fusion(f32[512,512]{1,0:T(8,128)} %copy-done.18, bf16[512,3072]{1,0:T(8,128)(2,1)} %bitcast.70, bf16[1,3072,512]{2,1,0:T(8,128)(2,1)S(1)} %copy-done, pred[]{:T(512)S(6)} %eq.31), kind=kOutput, calls=%fused_computation.36 | convolution fusion | flops 1610874880 | bytes 8388609 | tf_op jit(solution)/shard_map/dot_general | solution.py:346
  120.9 1.8 fusion.25
  123.6 2.1 fusion.16
  125.8 1.9 add_convert_fusion
  127.7 30.3 %shard_map.97 = bf16[2,16,3072]{2,1,0:T(8,128)(2,1)S(1)} custom-call(bf16[2,16,16,3072]{3,2,1,0:T(8,128)(2,1)S(1)} %bitcast.60), custom_call_target="tpu_custom_call" | custom-call | tf_op jit(solution)/shard_map/pallas_call | solution.py:332
  159.4 1.9 convolution_convert_fusion.8
  162.6 6.3 %collective-permute-done.3 = bf16[4,8,3072]{2,1,0:T(8,128)(2,1)S(1)} collective-permute-done((bf16[4,8,3072]{2,1,0:T(8,128)(2,1)S(1)}, bf16[4,8,3072]{2,1,0:T(8,128)(2,1)S(1)}, u32[]{:S(2)}, u32[]{:S(2)}) %collective-permute-start.3) | collective-permute-done | bytes 196640 | tf_op jit(solution)/shard_map/ppermute | solution.py:432
  169.6 24.4 %shard_map.98 = bf16[2,16,16,3072]{3,2,1,0:T(8,128)(2,1)} custom-call(bf16[2,16,3072]{2,1,0:T(8,128)(2,1)} %bitcast.75), custom_call_target="tpu_custom_call" | custom-call | tf_op jit(solution)/shard_map/pallas_call | solution.py:309
  194.1 3.3 %bitcast_select_fusion = bf16[512,3072]{1,0:T(8,128)(2,1)S(1)} fusion(bf16[2,16,16,3072]{3,2,1,0:T(8,128)(2,1)} %shard_map.98, pred[]{:T(512)S(6)} %eq.36, bf16[2,16,16,3072]{3,2,1,0:T(8,128)(2,1)} %shard_map.94), kind=kLoop, calls=%fused_computation.17 | loop fusion | flops 1572864 | bytes 9437185 | tf_op jit(solution)/shard_map/jit(_where)/select_n | solution.py:417
  200.7 1.8 fusion.6
  203.2 3.8 %fusion = bf16[1,3072,512]{2,1,0:T(8,128)(2,1)} fusion(bf16[512,3072]{1,0:T(8,128)(2,1)S(1)} %bitcast.72, bf16[512,3072]{1,0:T(8,128)(2,1)S(1)} %bitcast.68, pred[]{:T(512)S(6)} %eq.31, f32[512,512]{1,0:T(8,128)S(1)} %fusion.6, f32[512,512]{1,0:T(8,128)S(1)} %copy-done.5, f32[512,512]{1,0:T(8,128)S(1)} %copy-done.8), kind=kOutput, calls=%fused_computation.5 | convolution fusion | flops 1616379904 | bytes 12582913 | tf_op jit(solution)/shard_map/dot_general | solution.py:346
  207.0 3.8 %fusion.1 = bf16[1,3072,512]{2,1,0:T(8,128)(2,1)} fusion(bf16[512,3072]{1,0:T(8,128)(2,1)S(1)} %bitcast.73, bf16[512,3072]{1,0:T(8,128)(2,1)S(1)} %bitcast.69, pred[]{:T(512)S(6)} %eq.31, f32[512,512]{1,0:T(8,128)S(1)} %fusion.6, f32[512,512]{1,0:T(8,128)S(1)} %copy-done.5), kind=kOutput, calls=%fused_computation.6 | convolution fusion | flops 1615331328 | bytes 11534337 | tf_op jit(solution)/shard_map/dot_general | solution.py:346
  210.8 3.6 %fusion.2 = bf16[1,512,3072]{2,1,0:T(8,128)(2,1)} fusion(bf16[512,3072]{1,0:T(8,128)(2,1)S(1)} %bitcast_select_fusion, f32[512,512]{1,0:T(8,128)S(1)} %copy-done.8, f32[512,512]{1,0:T(8,128)S(1)} %copy-done.5), kind=kOutput, calls=%fused_computation.7 | convolution fusion | flops 1613758464 | bytes 8388608 | tf_op jit(solution)/shard_map/dot_general | solution.py:346
  (57 shorter events, 16.4 us)
Async XLA Ops:
  0.6 43.3 %copy-start = (bf16[1,3072,512]{2,1,0:T(8,128)(2,1)S(1)}, bf16[1,3072,512]{2,1,0:T(8,128)(2,1)}, u32[]{:S(2)}) copy-start(bf16[1,3072,512]{2,1,0:T(8,128)(2,1)} %param.11) | copy-start | bytes 9437188
  3.1 156.3 %collective-permute-start.2 = (bf16[4,32,8]{1,2,0:T(8,128)(2,1)}, bf16[4,32,8]{1,2,0:T(8,128)(2,1)}, u32[]{:S(2)}, u32[]{:S(2)}) collective-permute-start(bf16[4,32,8]{1,2,0:T(8,128)(2,1)} %fusion.63), channel_id=1, source_target_pairs={{0,16},{1,17},{2,18},{3,19},{4,20},{5,21},{6,22},{7,23},{8,24},{9,... | collective-permute-start | bytes 6152 | tf_op jit(solution)/shard_map/ppermute | solution.py:359
  8.5 69.9 %collective-permute-start = (bf16[4,32,8]{1,2,0:T(8,128)(2,1)}, bf16[4,32,8]{1,2,0:T(8,128)(2,1)}, u32[]{:S(2)}, u32[]{:S(2)}) collective-permute-start(bf16[4,32,8]{1,2,0:T(8,128)(2,1)} %fusion.63), channel_id=1, source_target_pairs={{16,0},{17,1},{18,2},{19,3},{20,4},{21,5},{22,6},{23,7},{24,8},{25... | collective-permute-start | bytes 6152 | tf_op jit(solution)/shard_map/ppermute | solution.py:358
  39.1 4.8 %copy-start.1 = (bf16[2,16,16,3072]{3,2,1,0:T(8,128)(2,1)S(1)}, bf16[2,16,16,3072]{3,2,1,0:T(8,128)(2,1)}, u32[]{:S(2)}) copy-start(bf16[2,16,16,3072]{3,2,1,0:T(8,128)(2,1)} %shard_map.94) | copy-start | bytes 9437188
  44.0 1.8 copy-start.16
  44.0 2.3 %copy-start.14 = (bf16[1,512,3072]{2,1,0:T(8,128)(2,1)S(1)}, bf16[1,512,3072]{2,1,0:T(8,128)(2,1)}, u32[]{:S(2)}) copy-start(bf16[1,512,3072]{2,1,0:T(8,128)(2,1)} %param.13) | copy-start | bytes 9437188
  46.2 1.8 copy-start.18
  80.8 10.6 %collective-permute-start.1 = (bf16[4,8,3072]{2,1,0:T(8,128)(2,1)}, bf16[4,8,3072]{2,1,0:T(8,128)(2,1)S(1)}, u32[]{:S(2)}, u32[]{:S(2)}) collective-permute-start(bf16[4,8,3072]{2,1,0:T(8,128)(2,1)} %convolution_convert_fusion.9), channel_id=1, source_target_pairs={{0,16},{1,17},{2,18},{3,19},{4,20},{5,21},{6,22},{7,23},{8,24},{9,... | collective-permute-start | bytes 589832 | tf_op jit(solution)/shard_map/ppermute | solution.py:400
  91.4 0.7 copy-start.12
  116.5 4.1 %copy-start.9 = (bf16[1,3072,512]{2,1,0:T(8,128)(2,1)S(1)}, bf16[1,3072,512]{2,1,0:T(8,128)(2,1)}, u32[]{:S(2)}) copy-start(bf16[1,3072,512]{2,1,0:T(8,128)(2,1)} %param.12) | copy-start | bytes 9437188
  116.5 4.1 %copy-start.10 = (bf16[2,16,16,3072]{3,2,1,0:T(8,128)(2,1)S(1)}, bf16[2,16,16,3072]{3,2,1,0:T(8,128)(2,1)}, u32[]{:S(2)}) copy-start(bf16[2,16,16,3072]{3,2,1,0:T(8,128)(2,1)} %shard_map.96) | copy-start | bytes 9437188
  116.5 4.3 %copy-start.17 = (f32[512,512]{1,0:T(8,128)S(1)}, f32[512,512]{1,0:T(8,128)}, u32[]{:S(2)}) copy-start(f32[512,512]{1,0:T(8,128)} %copy-done.16) | copy-start | bytes 3145732
  120.8 4.9 %copy-start.4 = (f32[512,512]{1,0:T(8,128)}, f32[512,512]{1,0:T(8,128)S(1)}, u32[]{:S(2)}) copy-start(f32[512,512]{1,0:T(8,128)S(1)} %fusion.22) | copy-start | bytes 3145732
  120.8 2.8 %copy-start.6 = (f32[512,512]{1,0:T(8,128)S(1)}, f32[512,512]{1,0:T(8,128)}, u32[]{:S(2)}) copy-start(f32[512,512]{1,0:T(8,128)} %fusion.8) | copy-start | bytes 3145732
  122.7 1.0 copy-start.7
  127.7 30.3 %copy-start.13 = (bf16[4,8,3072]{2,1,0:T(8,128)(2,1)S(1)}, bf16[4,8,3072]{2,1,0:T(8,128)(2,1)}, u32[]{:S(2)}) copy-start(bf16[4,8,3072]{2,1,0:T(8,128)(2,1)} %copy-done.12) | copy-start | bytes 589828
  161.3 7.6 %collective-permute-start.3 = (bf16[4,8,3072]{2,1,0:T(8,128)(2,1)S(1)}, bf16[4,8,3072]{2,1,0:T(8,128)(2,1)S(1)}, u32[]{:S(2)}, u32[]{:S(2)}) collective-permute-start(bf16[4,8,3072]{2,1,0:T(8,128)(2,1)S(1)} %convolution_convert_fusion.8), channel_id=1, source_target_pairs={{16,0},{17,1},{18,2},{19,3},{20,4},{21,5},{22,6},{23,7},{24,8},{25... | collective-permute-start | bytes 589832 | tf_op jit(solution)/shard_map/ppermute | solution.py:432
  194.1 3.7 %copy-start.2 = (bf16[2,16,16,3072]{3,2,1,0:T(8,128)(2,1)S(1)}, bf16[2,16,16,3072]{3,2,1,0:T(8,128)(2,1)}, u32[]{:S(2)}) copy-start(bf16[2,16,16,3072]{3,2,1,0:T(8,128)(2,1)} %shard_map.94) | copy-start | bytes 9437188
  194.1 4.7 %copy-start.3 = (bf16[2,16,16,3072]{3,2,1,0:T(8,128)(2,1)S(1)}, bf16[2,16,16,3072]{3,2,1,0:T(8,128)(2,1)}, u32[]{:S(2)}) copy-start(bf16[2,16,16,3072]{3,2,1,0:T(8,128)(2,1)} %shard_map.98) | copy-start | bytes 9437188
  198.8 1.9 copy-start.15
  200.7 1.8 copy-start.5
  200.7 1.8 copy-start.8
  200.7 2.5 %copy-start.11 = (bf16[2,16,16,3072]{3,2,1,0:T(8,128)(2,1)S(1)}, bf16[2,16,16,3072]{3,2,1,0:T(8,128)(2,1)}, u32[]{:S(2)}) copy-start(bf16[2,16,16,3072]{3,2,1,0:T(8,128)(2,1)} %shard_map.96) | copy-start | bytes 9437188

commit v4 on v3

--- a/solution.py
+++ b/solution.py
@@ -316,7 +316,9 @@
             pltpu.SemaphoreType.DMA((CHUNKS, slots, 4)),
             pltpu.SemaphoreType.DMA((CHUNKS, slots)),
         ],
-        compiler_params=pltpu.CompilerParams(collective_id=0, has_side_effects=True),
+        compiler_params=pltpu.CompilerParams(
+            collective_id=0, has_side_effects=True, vmem_limit_bytes=1024 * 1024
+        ),
     )(flat.reshape(CHUNKS, chunk, width))
     return got.reshape(-1, width)
 
@@ -336,7 +338,7 @@
         out_specs=pl.BlockSpec(memory_space=pltpu.VMEM),
         scratch_shapes=buffers + sems,
         compiler_params=pltpu.CompilerParams(
-            collective_id=1, has_side_effects=True, vmem_limit_bytes=32 * 1024 * 1024
+            collective_id=1, has_side_effects=True, vmem_limit_bytes=16 * 1024 * 1024
         ),
     )(partial.reshape(CHUNKS, SIDE * SIDE, rows, width))
     return summed.reshape(like.shape)
@@ -371,29 +373,21 @@
     first_grad = out_grad(last_rows)
     is_last = section == sections - 1
     own = current
-    all_rows = gate_pre = up_pre = all_grads = hidden_grad = None
+    all_rows = gate_pre = up_pre = all_grads = None
     for t in range(sections):
         active = section == t
         own = jnp.where(active, current, own)
-        own_f = current.astype(jnp.float32)
+        own_f = own.astype(jnp.float32)
         normed = (own_f * row_scale(own_f)).astype(jnp.bfloat16)
         send = jnp.where(is_last, first_grad, normed) if t == 0 and sections > 1 else normed
         got = gather(send)
         if t == 0:
             all_grads = got if sections > 1 else gather(first_grad)
-            hidden_grad = mm(all_grads, down_w, ((1,), (1,)))
-            all_rows = got
-            gate_pre = mm(got, gate_w)
-            up_pre = mm(got, up_w)
-            new_gate, new_up = gate_pre, up_pre
-        else:
-            new_gate, new_up = mm(got, gate_w), mm(got, up_w)
-            all_rows = jnp.where(active, got, all_rows)
-            gate_pre = jnp.where(active, new_gate, gate_pre)
-            up_pre = jnp.where(active, new_up, up_pre)
+        all_rows = got
+        gate_pre, up_pre = mm(got, gate_w), mm(got, up_w)
         if t < sections - 1:
-            partial = mm(activations(new_gate, new_up), down_w).astype(jnp.bfloat16)
-            back = scatter_sum(partial, current).astype(jnp.float32)
+            partial = mm(activations(gate_pre, up_pre), down_w).astype(jnp.bfloat16)
+            back = scatter_sum(partial, own).astype(jnp.float32)
             output_rows = (own_f + weights * back).astype(jnp.bfloat16)
             output = place(table, mask, output_rows, stream)
             if t == sections - 2:
@@ -410,12 +404,14 @@
     scale = row_scale(own_f)
 
     flow = upstream
+    own_grad = first_grad
+    all_grads, all_rows = lax.optimization_barrier((all_grads, all_rows))
     for t in reversed(range(sections)):
         active = section == t
         if t < sections - 1:
-            got = gather(out_grad(grads_in))
-            all_grads = jnp.where(active, got, all_grads)
-            hidden_grad = mm(all_grads, down_w, ((1,), (1,)))
+            own_grad = jnp.where(active, out_grad(grads_in), own_grad)
+            all_grads = gather(own_grad)
+        hidden_grad = mm(all_grads, down_w, ((1,), (1,)))
         gate_units = (hidden_grad * slope).astype(jnp.bfloat16)
         up_units = (hidden_grad * silu_val).astype(jnp.bfloat16)
         if t > 0:

time: 215 us -> 203 us (0.944)
  other arithmetic: 9.95 us -> 5.92 us
  matrix products: 44.9 us -> 41.8 us
  starting transfers between devices: 12.9 us -> 9.86 us
    dot_general x12 -> x11, matrix products: 37 us -> 33.2 us  [mm(): lax.dot_general(a, b, (dims, ((), ())), preferred_element_type=jnp.float32)]
    ppermute x1, starting transfers between devices: 5.43 us -> 1.88 us  [shards(): previous_table = lax.ppermute(table, 'section', up_route)]
    pallas_call x3, Pallas kernels: 73.1 us -> 69.7 us  [gather(): pl.pallas_call(gather_kernel, out_shape=jax.ShapeDtypeStruct((CHUNKS, slo...]
    select_n x2 -> x1, other arithmetic: 3.64 us -> 1.12 us  [shards(): own_grad = jnp.where(active, out_grad(grads_in), own_grad)]
    unnamed x38 -> x28, local copies, waits for them, and re-layouts: 5.79 us -> 4.99 us
  transfers between devices with their start and end apart: 4 -> 4, of which waited for: 1 -> 2; matrix products, arithmetic and copies ran while one was open for 15% -> 13% of each run, Pallas kernels for 51% -> 54%
where the time goes in v4:
time: 203 us
  Pallas kernels  132 us (65%)
  matrix products  41.8 us (21%)
  starting transfers between devices  9.86 us (5%)
  waiting for transfers between devices  8.12 us (4%)
  other arithmetic  5.92 us (3%)
  local copies, waits for them, and re-layouts  4.99 us (2%)
    pallas_call x3, Pallas kernels, gather(): pl.pallas_call(gather_kernel, out_shape=jax.ShapeDtypeStruct((CHUNKS, slo...  69.7 us
    pallas_call x2, Pallas kernels, scatter_sum(): pl.pallas_call(scatter_kernel, out_shape=jax.ShapeDtypeStruct((CHUNKS, ro...  61.8 us
    dot_general x11, matrix products, mm(): lax.dot_general(a, b, (dims, ((), ())), preferred_element_type=jnp.float32)  33.2 us
    dot_general x4, matrix products, pick(): lax.dot_general(table, values, (((1,), (1,)), ((0,), (0,))), preferred_el...  8.58 us
    ppermute x1, waiting for transfers between devices, shards(): grads_in = lax.ppermute(pick(previous_table, result), 'section', down_route)  6.46 us
    ppermute x1, starting transfers between devices, shards(): current = lax.ppermute(pick(next_table, output), 'section', up_route)  5.42 us
    unnamed x28, local copies, waits for them, and re-layouts  4.99 us
  transfers between devices with their start and end apart: 4, of which 2 were waited for; matrix products, arithmetic and copies ran while one was open for 13% of the time, Pallas kernels for 54%

profile of v4, /device:TPU:0, one launch (start us, length us, event | category | flops | bytes accessed | tf_op | source)
XLA Modules:
  0.0 203.1 jit_solution(9323686002419949460)
XLA Ops:
  6.6 2.3 %fusion.47 = (bf16[4,8,3072]{2,1,0:T(8,128)(2,1)S(1)}, f32[4,8,3072]{2,1,0:T(8,128)}) fusion(bf16[4,8,3072]{2,1,0:T(8,128)(2,1)S(1)} %get-tuple-element.12, f32[4,8]{1,0:T(4,128)S(1)} %add_rsqrt_fusion.1, pred[]{:T(512)S(6)} %eq.31, f32[4,8]{1,0:T(4,128)S(1)} %multiply_reduce_fusion, bf16[4,32,3072]{2,1,0:T(8,128)(2,1)} %param.8, ...), kind=kOutput, calls=%fused_computation.68 | convolution fusion | flops 7079936 | bytes 1573761 | tf_op jit(solution)/shard_map/dot_general | solution.py:24
  8.9 24.8 %shard_map.94 = bf16[2,16,16,3072]{3,2,1,0:T(8,128)(2,1)S(1)} custom-call(bf16[2,16,3072]{2,1,0:T(8,128)(2,1)S(1)} %bitcast.77), custom_call_target="tpu_custom_call" | custom-call | tf_op jit(solution)/shard_map/pallas_call | solution.py:309
  35.3 2.8 %fusion.20 = f32[512,512]{1,0:T(8,128)} fusion(bf16[512,3072]{1,0:T(8,128)(2,1)S(1)} %bitcast.68, bf16[1,3072,512]{2,1,0:T(8,128)(2,1)S(1)} %copy-done.10), kind=kOutput, calls=%fused_computation.31 | convolution fusion | flops 1610612736 | bytes 7340032 | tf_op jit(solution)/shard_map/dot_general | solution.py:348
  38.1 8.4 %convolution_convert_fusion.3 = bf16[512,3072]{1,0:T(8,128)(2,1)} fusion(bf16[1,512,3072]{2,1,0:T(8,128)(2,1)} %param.13, bf16[512,3072]{1,0:T(8,128)(2,1)} %bitcast.69, bf16[1,3072,512]{2,1,0:T(8,128)(2,1)S(1)} %copy-done, f32[512,512]{1,0:T(8,128)} %fusion.20), kind=kOutput, calls=%fused_computation.4 | convolution fusion | flops 3224371200 | bytes 13631488 | tf_op jit(solution)/shard_map/dot_general | solution.py:348
  46.5 1.9 copy-done.5
  48.3 30.9 %shard_map.95 = bf16[2,16,3072]{2,1,0:T(8,128)(2,1)S(1)} custom-call(bf16[2,16,16,3072]{3,2,1,0:T(8,128)(2,1)S(1)} %bitcast.71), custom_call_target="tpu_custom_call" | custom-call | tf_op jit(solution)/shard_map/pallas_call | solution.py:334
  79.3 2.4 %convolution_convert_fusion.9 = bf16[4,8,3072]{2,1,0:T(8,128)(2,1)} fusion(bf16[4,32,8]{1,2,0:T(8,128)(2,1)} %collective-permute-done, bf16[4,32,3072]{2,1,0:T(8,128)(2,1)} %param.7, pred[4,32]{1,0:T(4,128)(4,1)S(1)} %broadcast_compare_fusion, bf16[4,8,3072]{2,1,0:T(8,128)(2,1)S(1)} %get-tuple-element.12, bf16[4,8,3072]{2,1,0:T(8,128)(2,1)S(1)} %bitcast.74, ...), kind=kOutput, calls=%fused_computation.16 | convolution fusion | flops 13961216 | bytes 1379072 | tf_op jit(solution)/shard_map/dot_general | solution.py:24
  81.7 5.4 %collective-permute-start.1 = (bf16[4,8,3072]{2,1,0:T(8,128)(2,1)}, bf16[4,8,3072]{2,1,0:T(8,128)(2,1)S(1)}, u32[]{:S(2)}, u32[]{:S(2)}) collective-permute-start(bf16[4,8,3072]{2,1,0:T(8,128)(2,1)} %convolution_convert_fusion.9), channel_id=1, source_target_pairs={{0,16},{1,17},{2,18},{3,19},{4,20},{5,21},{6,22},{7,23},{8,24},{9,... | collective-permute-start | bytes 589832 | tf_op jit(solution)/shard_map/ppermute | solution.py:394
  87.1 1.9 collective-permute-start.2
  89.0 1.7 collective-permute-done.1
  91.5 22.2 %shard_map.96 = bf16[2,16,16,3072]{3,2,1,0:T(8,128)(2,1)S(1)} custom-call(bf16[2,16,3072]{2,1,0:T(8,128)(2,1)S(1)} %bitcast.75), custom_call_target="tpu_custom_call" | custom-call | tf_op jit(solution)/shard_map/pallas_call | solution.py:309
  113.8 1.8 fusion.18
  115.6 1.8 fusion.12
  118.8 1.8 fusion.8
  120.7 2.1 %fusion.16 = f32[512,3072]{1,0:T(8,128)S(1)} fusion(bf16[1,3072,512]{2,1,0:T(8,128)(2,1)S(1)} %copy-done.11, f32[512,512]{1,0:T(8,128)S(1)} %fusion.8, f32[512,512]{1,0:T(8,128)S(1)} %fusion.18, f32[512,512]{1,0:T(8,128)S(1)} %fusion.12), kind=kOutput, calls=%fused_computation.27 | convolution fusion | flops 1613234176 | bytes 12582912 | tf_op jit(solution)/shard_map/dot_general | solution.py:348
  122.8 1.9 add_convert_fusion
  124.7 30.8 %shard_map.97 = bf16[2,16,3072]{2,1,0:T(8,128)(2,1)S(1)} custom-call(bf16[2,16,16,3072]{3,2,1,0:T(8,128)(2,1)S(1)} %bitcast.61), custom_call_target="tpu_custom_call" | custom-call | tf_op jit(solution)/shard_map/pallas_call | solution.py:334
  156.3 2.5 %convolution_convert_fusion.8 = bf16[4,8,3072]{2,1,0:T(8,128)(2,1)} fusion(bf16[4,32,8]{1,2,0:T(8,128)(2,1)} %collective-permute-done.2, bf16[4,32,3072]{2,1,0:T(8,128)(2,1)} %param.8, pred[4,32]{1,0:T(4,128)(4,1)S(1)} %broadcast_compare_fusion, f32[4,8,3072]{2,1,0:T(8,128)} %get-tuple-element.14, bf16[4,8,3072]{2,1,0:T(8,128)(2,1)S(1)} %bitcast.73, ...), kind=kOutput, calls=%fused_computation.15 | convolution fusion | flops 14256128 | bytes 1772544 | tf_op jit(solution)/shard_map/dot_general | solution.py:24
  160.1 6.5 %collective-permute-done.3 = bf16[4,8,3072]{2,1,0:T(8,128)(2,1)S(1)} collective-permute-done((bf16[4,8,3072]{2,1,0:T(8,128)(2,1)}, bf16[4,8,3072]{2,1,0:T(8,128)(2,1)S(1)}, u32[]{:S(2)}, u32[]{:S(2)}) %collective-permute-start.3) | collective-permute-done | bytes 196640 | tf_op jit(solution)/shard_map/ppermute | solution.py:428
  167.7 22.7 %shard_map.98 = bf16[2,16,16,3072]{3,2,1,0:T(8,128)(2,1)S(1)} custom-call(bf16[2,16,3072]{2,1,0:T(8,128)(2,1)S(1)} %bitcast.76), custom_call_target="tpu_custom_call" | custom-call | tf_op jit(solution)/shard_map/pallas_call | solution.py:309
  190.4 1.8 fusion.6
  192.3 3.6 %fusion.2 = bf16[1,512,3072]{2,1,0:T(8,128)(2,1)} fusion(bf16[512,3072]{1,0:T(8,128)(2,1)S(1)} %bitcast.63, f32[512,512]{1,0:T(8,128)S(1)} %copy-done.9, f32[512,512]{1,0:T(8,128)S(1)} %copy-done.7), kind=kOutput, calls=%fused_computation.7 | convolution fusion | flops 1613758464 | bytes 8388608 | tf_op jit(solution)/shard_map/dot_general | solution.py:348
  195.9 3.7 %fusion = bf16[1,3072,512]{2,1,0:T(8,128)(2,1)} fusion(bf16[512,3072]{1,0:T(8,128)(2,1)S(1)} %bitcast.66, f32[512,512]{1,0:T(8,128)S(1)} %fusion.6, f32[512,512]{1,0:T(8,128)S(1)} %copy-done.7, f32[512,512]{1,0:T(8,128)S(1)} %copy-done.9), kind=kOutput, calls=%fused_computation.5 | convolution fusion | flops 1614807040 | bytes 9437184 | tf_op jit(solution)/shard_map/dot_general | solution.py:348
  199.5 3.6 %fusion.1 = bf16[1,3072,512]{2,1,0:T(8,128)(2,1)} fusion(bf16[512,3072]{1,0:T(8,128)(2,1)S(1)} %bitcast.67, f32[512,512]{1,0:T(8,128)S(1)} %fusion.6, f32[512,512]{1,0:T(8,128)S(1)} %copy-done.7), kind=kOutput, calls=%fused_computation.6 | convolution fusion | flops 1613758464 | bytes 8388608 | tf_op jit(solution)/shard_map/dot_general | solution.py:348
  (44 shorter events, 13.0 us)
Async XLA Ops:
  0.6 37.5 %copy-start = (bf16[1,3072,512]{2,1,0:T(8,128)(2,1)S(1)}, bf16[1,3072,512]{2,1,0:T(8,128)(2,1)}, u32[]{:S(2)}) copy-start(bf16[1,3072,512]{2,1,0:T(8,128)(2,1)} %param.12) | copy-start | bytes 9437188
  3.1 76.2 %collective-permute-start = (bf16[4,32,8]{1,2,0:T(8,128)(2,1)}, bf16[4,32,8]{1,2,0:T(8,128)(2,1)}, u32[]{:S(2)}, u32[]{:S(2)}) collective-permute-start(bf16[4,32,8]{1,2,0:T(8,128)(2,1)} %fusion.65), channel_id=1, source_target_pairs={{16,0},{17,1},{18,2},{19,3},{20,4},{21,5},{22,6},{23,7},{24,8},{25... | collective-permute-start | bytes 6152 | tf_op jit(solution)/shard_map/ppermute | solution.py:360
  6.6 28.7 %copy-start.10 = (bf16[1,3072,512]{2,1,0:T(8,128)(2,1)S(1)}, bf16[1,3072,512]{2,1,0:T(8,128)(2,1)}, u32[]{:S(2)}) copy-start(bf16[1,3072,512]{2,1,0:T(8,128)(2,1)} %param.11) | copy-start | bytes 9437188
  33.7 1.7 copy-start.3
  46.4 1.9 copy-start.5
  81.7 32.1 %copy-start.11 = (bf16[1,3072,512]{2,1,0:T(8,128)(2,1)S(1)}, bf16[1,3072,512]{2,1,0:T(8,128)(2,1)}, u32[]{:S(2)}) copy-start(bf16[1,3072,512]{2,1,0:T(8,128)(2,1)} %param.11) | copy-start | bytes 9437188
  81.7 9.0 %collective-permute-start.1 = (bf16[4,8,3072]{2,1,0:T(8,128)(2,1)}, bf16[4,8,3072]{2,1,0:T(8,128)(2,1)S(1)}, u32[]{:S(2)}, u32[]{:S(2)}) collective-permute-start(bf16[4,8,3072]{2,1,0:T(8,128)(2,1)} %convolution_convert_fusion.9), channel_id=1, source_target_pairs={{0,16},{1,17},{2,18},{3,19},{4,20},{5,21},{6,22},{7,23},{8,24},{9,... | collective-permute-start | bytes 589832 | tf_op jit(solution)/shard_map/ppermute | solution.py:394
  87.1 69.2 %collective-permute-start.2 = (bf16[4,32,8]{1,2,0:T(8,128)(2,1)}, bf16[4,32,8]{1,2,0:T(8,128)(2,1)}, u32[]{:S(2)}, u32[]{:S(2)}) collective-permute-start(bf16[4,32,8]{1,2,0:T(8,128)(2,1)} %fusion.65), channel_id=1, source_target_pairs={{0,16},{1,17},{2,18},{3,19},{4,20},{5,21},{6,22},{7,23},{8,24},{9,... | collective-permute-start | bytes 6152 | tf_op jit(solution)/shard_map/ppermute | solution.py:361
  113.7 1.8 copy-start.1
  115.6 7.2 %copy-start.6 = (f32[512,512]{1,0:T(8,128)}, f32[512,512]{1,0:T(8,128)S(1)}, u32[]{:S(2)}) copy-start(f32[512,512]{1,0:T(8,128)S(1)} %fusion.18) | copy-start | bytes 3145732
  115.6 2.3 %copy-start.4 = (bf16[2,16,16,3072]{3,2,1,0:T(8,128)(2,1)S(1)}, bf16[2,16,16,3072]{3,2,1,0:T(8,128)(2,1)}, u32[]{:S(2)}) copy-start(bf16[2,16,16,3072]{3,2,1,0:T(8,128)(2,1)} %copy-done.3) | copy-start | bytes 9437188
  115.6 3.2 %copy-start.12 = (bf16[1,512,3072]{2,1,0:T(8,128)(2,1)S(1)}, bf16[1,512,3072]{2,1,0:T(8,128)(2,1)}, u32[]{:S(2)}) copy-start(bf16[1,512,3072]{2,1,0:T(8,128)(2,1)} %param.13) | copy-start | bytes 9437188
  118.8 1.8 copy-start.8
  158.8 7.8 %collective-permute-start.3 = (bf16[4,8,3072]{2,1,0:T(8,128)(2,1)}, bf16[4,8,3072]{2,1,0:T(8,128)(2,1)S(1)}, u32[]{:S(2)}, u32[]{:S(2)}) collective-permute-start(bf16[4,8,3072]{2,1,0:T(8,128)(2,1)} %convolution_convert_fusion.8), channel_id=1, source_target_pairs={{16,0},{17,1},{18,2},{19,3},{20,4},{21,5},{22,6},{23,7},{24,8},{25... | collective-permute-start | bytes 589832 | tf_op jit(solution)/shard_map/ppermute | solution.py:428
  160.1 30.3 %copy-start.13 = (bf16[1,512,3072]{2,1,0:T(8,128)(2,1)S(1)}, bf16[1,512,3072]{2,1,0:T(8,128)(2,1)}, u32[]{:S(2)}) copy-start(bf16[1,512,3072]{2,1,0:T(8,128)(2,1)} %param.13) | copy-start | bytes 9437188
  190.4 1.9 copy-start.7
  190.4 1.8 copy-start.9
  192.3 3.6 %copy-start.2 = (bf16[2,16,16,3072]{3,2,1,0:T(8,128)(2,1)S(1)}, bf16[2,16,16,3072]{3,2,1,0:T(8,128)(2,1)}, u32[]{:S(2)}) copy-start(bf16[2,16,16,3072]{3,2,1,0:T(8,128)(2,1)} %copy-done.1) | copy-start | bytes 9437188
